TPU v7x, 128 devices: a whole 4x4x4 slice. The times are simulated.
128 devices in a mesh: grp: 4 (over x), dev: 32 (over z, y, core).
Axes of the slice: x: 4, y: 4, z: 4, core: 2. Of those that a mesh axis runs over, the one named last changes fastest.
Arguments:
- memory: bfloat16 [262144, 512], P(('grp', 'dev')), may hold values from -6 to 6
- event_nodes: int32 [16384, 2], P(('grp', 'dev')), may hold values from 0 to 262143, as said below
- event_ticks: int32 [16384], P(('grp', 'dev')), may hold values from 0 to 99999
- neighbour_ids: int32 [16384, 20], P(('grp', 'dev')), may hold values from 0 to 262143, as said below
- neighbour_ticks: int32 [16384, 20], P(('grp', 'dev')), may hold values from 0 to 99999
- freq: float32 [128], replicated, may hold values from 1e-05 to 1
- phase: float32 [128], replicated, may hold values from -3.140625 to 3.140625
- w_msg1: bfloat16 [1152, 1024], replicated, may hold values from -0.1875 to 0.1875
- b_msg1: float32 [1024], replicated, may hold values from -3 to 3
- w_msg2: bfloat16 [1024, 512], replicated, may hold values from -0.1875 to 0.1875
- b_msg2: float32 [512], replicated, may hold values from -3 to 3
- w_query: bfloat16 [512, 512], replicated, may hold values from -1 to 1
- w_keyval: bfloat16 [640, 1024], replicated, may hold values from -1 to 1
- w_out: bfloat16 [512, 512], replicated, may hold values from -0.25 to 0.25
- gru_input: bfloat16 [512, 1536], replicated, may hold values from -0.25 to 0.25
- gru_hidden: bfloat16 [512, 1536], replicated, may hold values from -0.25 to 0.25
- gru_bias: float32 [2, 1536], replicated, may hold values from -3 to 3
Outputs:
- embedding: bfloat16 [16384, 512], P(('grp', 'dev'))
- new_memory: bfloat16 [262144, 512], P(('grp', 'dev'))
Inputs may be any that keep to these rules, and one draw needn't show every extreme that they name: `event_nodes`: node n is held by device n // 2048 of the grp-major order; of the 256 ids of one device's events, at most 4 belong to any one owner device. `neighbour_ids`: of the 2560 neighbour ids of one device's events, at most 40 belong to any one owner device.
All inputs are finite; a program needn't handle non-finite values.
Results may differ from a plain program's by a relative error of at most 0.01.
Values may be sent and summed in bfloat16 or wider, within the bound.
No kernel may reach another device: no remote copies, remote signals or barrier semaphores. Data moves between devices by JAX's collectives and lax.ppermute only.
A program may use at most 128 MiB of HBM per device.

v0:
```python
import jax
import jax.numpy as jnp
from jax import lax
from jax.sharding import PartitionSpec as P

HDIM = 128


def encode(ticks, freq, phase):
    return jnp.cos(ticks.astype(jnp.float32)[..., None] * freq + phase).astype(jnp.bfloat16)


def take_rows(table, indices):
    flat = jnp.take(table, indices.reshape(-1), axis=0, mode="clip")
    return flat.reshape(indices.shape + (table.shape[1],))


def placing(node_ids, capacity, node_dev, owners):
    owner = node_ids // node_dev
    local_rows = node_ids % node_dev
    onehot = (owner[:, None] == jnp.arange(owners, dtype=jnp.int32)[None, :]).astype(jnp.int32)
    slot = jnp.sum(jnp.cumsum(onehot, axis=0) * onehot, axis=1) - 1
    position = owner * capacity + slot
    request = jnp.full((owners * capacity,), -1, jnp.int32).at[position].set(local_rows)
    return (position, request.reshape(owners, capacity))


def on_device(
    memory,
    event_nodes,
    event_ticks,
    neighbour_ids,
    neighbour_ticks,
    freq,
    phase,
    w_msg1,
    b_msg1,
    w_msg2,
    b_msg2,
    w_query,
    w_keyval,
    w_out,
    gru_input,
    gru_hidden,
    gru_bias,
):
    owners = lax.axis_size(("grp", "dev"))
    node_dev, width = memory.shape
    events = event_nodes.shape[0]
    fanout = neighbour_ids.shape[1]
    cap_e = 4 * events // owners
    cap_n = 2 * fanout * events // owners
    event_pos, event_req = placing(event_nodes.reshape(-1), cap_e, node_dev, owners)
    received = lax.all_to_all(event_req, ("grp", "dev"), split_axis=0, concat_axis=0, tiled=True)
    rows = take_rows(memory, received)
    event_rows = lax.all_to_all(rows, ("grp", "dev"), split_axis=0, concat_axis=0, tiled=True)
    pair = take_rows(event_rows.reshape(owners * cap_e, width), event_pos).reshape(events, 2, width)
    m_src = pair[:, 0]
    m_dst = pair[:, 1]
    enc = encode(event_ticks, freq, phase)
    inputs = jnp.concatenate(
        [
            jnp.concatenate([m_src, m_dst, enc], axis=1),
            jnp.concatenate([m_dst, m_src, enc], axis=1),
        ],
        axis=0,
    )
    hidden = jnp.maximum(
        jnp.dot(inputs, w_msg1, preferred_element_type=jnp.float32) + b_msg1, 0.0
    ).astype(jnp.bfloat16)
    messages = (jnp.dot(hidden, w_msg2, preferred_element_type=jnp.float32) + b_msg2).astype(
        jnp.bfloat16
    )
    paired_msgs = jnp.stack([messages[:events], messages[events:]], axis=1).reshape(
        2 * events, width
    )
    source_of_slot = (
        jnp.zeros((owners * cap_e,), jnp.int32)
        .at[event_pos]
        .set(jnp.arange(2 * events, dtype=jnp.int32))
    )
    outgoing = take_rows(paired_msgs, source_of_slot).reshape(owners, cap_e, width)
    arrived = lax.all_to_all(outgoing, ("grp", "dev"), split_axis=0, concat_axis=0, tiled=True)
    valid = (received >= 0).reshape(-1)
    target = jnp.maximum(received, 0).reshape(-1)
    terms = jnp.where(valid[:, None], arrived.reshape(-1, width).astype(jnp.float32), 0.0)
    sums = jnp.zeros((node_dev, width), jnp.float32).at[target].add(terms)
    counts = jnp.zeros((node_dev,), jnp.float32).at[target].add(valid.astype(jnp.float32))
    mean = (sums / jnp.maximum(counts, 1.0)[:, None]).astype(jnp.bfloat16)
    gate_in = jnp.dot(mean, gru_input, preferred_element_type=jnp.float32) + gru_bias[0]
    gate_hid = jnp.dot(memory, gru_hidden, preferred_element_type=jnp.float32) + gru_bias[1]
    reset = jax.nn.sigmoid(gate_in[:, :width] + gate_hid[:, :width])
    update = jax.nn.sigmoid(gate_in[:, width : 2 * width] + gate_hid[:, width : 2 * width])
    candidate = jnp.tanh(gate_in[:, 2 * width :] + reset * gate_hid[:, 2 * width :])
    fresh = (1.0 - update) * candidate + update * memory.astype(jnp.float32)
    new_memory = jnp.where(counts[:, None] > 0.0, fresh, memory.astype(jnp.float32)).astype(
        jnp.bfloat16
    )
    near_pos, near_req = placing(neighbour_ids.reshape(-1), cap_n, node_dev, owners)
    rows = take_rows(
        memory, lax.all_to_all(near_req, ("grp", "dev"), split_axis=0, concat_axis=0, tiled=True)
    )
    near_rows = lax.all_to_all(
        rows, ("grp", "dev"), split_axis=0, concat_axis=0, tiled=True
    ).reshape(owners * cap_n, width)
    m_near = take_rows(near_rows, near_pos).reshape(events, fanout, width)
    heads = width // HDIM
    query = (
        jnp.dot(m_src, w_query, preferred_element_type=jnp.float32)
        .astype(jnp.bfloat16)
        .reshape(events, heads, HDIM)
    )
    block = min(events, 128)
    blocks = events // block

    def embed_block(args):
        query_block, near_block, ticks_block, near_ticks = args
        dt_enc = encode(ticks_block[:, None] - near_ticks, freq, phase)
        feats = jnp.concatenate([near_block, dt_enc], axis=-1).reshape(block * fanout, -1)
        keyval = (
            jnp.dot(feats, w_keyval, preferred_element_type=jnp.float32)
            .astype(jnp.bfloat16)
            .reshape(block, fanout, 2, heads, HDIM)
        )
        scores = jnp.einsum(
            "ehc,ekhc->ehk", query_block, keyval[:, :, 0], preferred_element_type=jnp.float32
        ) / jnp.sqrt(jnp.float32(HDIM))
        scores = scores - jnp.max(scores, axis=-1, keepdims=True)
        expo = jnp.exp(scores)
        weights = (expo / jnp.sum(expo, axis=-1, keepdims=True)).astype(jnp.bfloat16)
        attn = (
            jnp.einsum(
                "ehk,ekhc->ehc", weights, keyval[:, :, 1], preferred_element_type=jnp.float32
            )
            .astype(jnp.bfloat16)
            .reshape(block, width)
        )
        return jnp.dot(attn, w_out, preferred_element_type=jnp.float32).astype(jnp.bfloat16)

    embedding = lax.map(
        embed_block,
        (
            query.reshape(blocks, block, heads, HDIM),
            m_near.reshape(blocks, block, fanout, width),
            event_ticks.reshape(blocks, block),
            neighbour_ticks.reshape(blocks, block, fanout),
        ),
    ).reshape(events, width)
    return (embedding, new_memory)


def solution(mesh):
    in_specs = (
        P(("grp", "dev"), None),
        P(("grp", "dev"), None),
        P(("grp", "dev")),
        P(("grp", "dev"), None),
        P(("grp", "dev"), None),
        P(),
        P(),
        P(),
        P(),
        P(),
        P(),
        P(),
        P(),
        P(),
        P(),
        P(),
        P(),
    )
    out_specs = (P(("grp", "dev"), None), P(("grp", "dev"), None))
    return jax.shard_map(
        on_device, mesh=mesh, in_specs=in_specs, out_specs=out_specs, check_vma=False
    )
```

profile of v0, /device:TPU:1, one launch (start us, length us, event | category | flops | bytes accessed | tf_op | source)
XLA Modules:
  0.0 225.8 jit_solution(6563300145811556233)
XLA Ops:
  3.2 1.4 scatter_custom_fusion
  5.3 11.5 %all-to-all-start = ((s32[128,1,4]{2,1,0:T(1,128)}), s32[128,1,4]{2,1,0:T(1,128)S(1)}, u32[]{:S(2)}, u32[]{:S(2)}) async-start(s32[128,1,4]{2,1,0:T(1,128)} %bitcast.5), calls=%async_computation | async-start | bytes 131072 | tf_op jit(solution)/shard_map/all_to_all | solution.py:54
  20.3 1.5 broadcast_add_fusion
  22.1 1.6 fusion.26
  25.5 1.9 scatter_custom_fusion.3
  29.2 3.8 %gather_fusion = bf16[512,512]{1,0:T(8,128)(2,1)S(1)} fusion(bf16[2048,512]{1,0:T(8,128)(2,1)} %param.17, s32[1024]{0:T(1024)S(1)} %pad_clamp_fusion.3), kind=kCustom, calls=%fused_computation | custom fusion | bytes 1050624 | tf_op jit(solution)/shard_map/jit(_take)/gather | solution.py:14
  34.0 9.8 %all-to-all-start.1 = ((bf16[128,4,512]{2,1,0:T(4,128)(2,1)}), bf16[128,4,512]{2,1,0:T(4,128)(2,1)S(1)}, u32[]{:S(2)}, u32[]{:S(2)}) async-start(bf16[128,4,512]{2,1,0:T(4,128)(2,1)} %reshape.410), calls=%async_computation.1 | async-start | bytes 1048576 | tf_op jit(solution)/shard_map/all_to_all | solution.py:56
  44.6 10.1 %scatter_custom_fusion.1 = s32[5120]{0:T(1024)S(1)} fusion(s32[2560]{0:T(1024)S(1)} %get-tuple-element.27, s32[2560]{0:T(1024)} %get-tuple-element.46, s32[]{:T(128)} %constant.93.clone.1), kind=kCustom, calls=%fused_computation.125 | custom fusion | bytes 20992 | tf_op jit(solution)/shard_map/scatter | solution.py:24
  56.1 1.2 pad_clamp_fusion.2
  57.3 1.6 cosine_convert_fusion.1
  58.9 10.2 %all-to-all-start.2 = ((s32[128,1,40]{2,1,0:T(1,128)}), s32[128,1,40]{2,1,0:T(1,128)}, u32[]{:S(2)}, u32[]{:S(2)}) async-start(s32[128,1,40]{2,1,0:T(1,128)} %bitcast.11), calls=%async_computation.2 | async-start | bytes 131072 | tf_op jit(solution)/shard_map/all_to_all | solution.py:101
  69.3 1.4 gather_fusion.1
  71.3 2.3 %fusion.28 = bf16[256,512]{1,0:T(8,128)(2,1)S(1)} fusion(bf16[1024,512]{1,0:T(8,128)(2,1)} %param.26, bf16[1152,1024]{1,0:T(8,128)(2,1)S(1)} %copy-done, bf16[128,128]{1,0:T(8,128)(2,1)S(1)} %copy-done.9, bf16[128,512]{1,0:T(8,128)(2,1)S(1)} %get-tuple-element.51, bf16[128,512]{1,0:T(8,128)(2,1)S(1)} %get-tuple-element.50, f32[1024]{0:T(1024)S(1)} %copy-done.17, ...), kind=kOutput, calls=%fused_computation.55 | convolution fusion | flops 877002752 | bytes 3971072 | tf_op jit(solution)/shard_map/dot_general | solution.py:71
  74.1 2.0 gather_fusion.4
  77.0 1.5 all-to-all-done.2
  78.4 8.3 %all-to-all-start.4 = ((bf16[128,4,512]{2,1,0:T(4,128)(2,1)}), bf16[128,4,512]{2,1,0:T(4,128)(2,1)S(1)}, u32[]{:S(2)}, u32[]{:S(2)}) async-start(bf16[128,4,512]{2,1,0:T(4,128)(2,1)} %reshape.422), calls=%async_computation.4 | async-start | bytes 1048576 | tf_op jit(solution)/shard_map/all_to_all | solution.py:83
  86.7 1.7 reduce.20
  88.6 21.4 %gather_fusion.2 = bf16[5120,512]{1,0:T(8,128)(2,1)} fusion(bf16[2048,512]{1,0:T(8,128)(2,1)S(1)} %copy-done.2, s32[5120]{0:T(1024)S(1)} %broadcast_clamp_fusion), kind=kCustom, calls=%fused_computation.2 | custom fusion | bytes 10506240 | tf_op jit(solution)/shard_map/jit(_take)/gather | solution.py:14
  110.7 10.2 %all-to-all-start.3 = ((bf16[128,40,512]{2,1,0:T(8,128)(2,1)}), bf16[128,40,512]{2,1,0:T(8,128)(2,1)}, u32[]{:S(2)}, u32[]{:S(2)}) async-start(bf16[128,40,512]{2,1,0:T(8,128)(2,1)} %bitcast.73), calls=%async_computation.3 | async-start | bytes 10485760 | tf_op jit(solution)/shard_map/all_to_all | solution.py:103
  121.2 5.7 %cosine_convert_fusion = bf16[2560,128]{1,0:T(8,128)(2,1)} fusion(f32[128]{0:T(128)S(1)} %copy-done.12, f32[128]{0:T(128)S(1)} %copy-done.13, f32[2560]{0:T(1024)S(1)} %mul.91), kind=kLoop, calls=%fused_computation.51 | loop fusion | flops 983040 | bytes 666624 | tf_op jit(solution)/shard_map/while/body/eval_jaxpr/convert_element_type | solution.py:10
  126.9 7.8 %convolution_add_fusion = f32[2048,1536]{1,0:T(8,128)} fusion(bf16[2048,512]{1,0:T(8,128)(2,1)S(1)} %copy-done.2, bf16[512,1536]{1,0:T(8,128)(2,1)} %param.32, f32[1536]{0:T(1024)S(1)} %get-tuple-element.25), kind=kOutput, calls=%fused_computation.10 | convolution fusion | flops 3224371200 | bytes 16259072 | tf_op jit(solution)/shard_map/dot_general | solution.py:91
  135.2 3.5 %scatter_custom_fusion.2 = f32[2048]{0:T(1024)S(1)} fusion(s32[512]{0:T(512)S(1)} %reshape.482, f32[512]{0:T(512)S(1)} %convert_element_type.80, f32[]{:T(128)} %constant.105.clone.1), kind=kCustom, calls=%fused_computation.137 | custom fusion | flops 512 | bytes 8196 | tf_op jit(solution)/shard_map/scatter-add | solution.py:88
  140.8 6.0 %scatter_custom_fusion.4 = f32[2048,512]{1,0:T(8,128)} fusion(s32[512]{0:T(512)S(1)} %reshape.482, f32[]{:T(128)} %constant.105.clone.1, f32[512,512]{1,0:T(8,128)S(1)} %reshape.423, pred[512]{0:T(512)(128)(4,1)S(1)} %ge.12), kind=kCustom, calls=%fused_computation.42 | custom fusion | flops 524288 | bytes 5244416 | tf_op jit(solution)/shard_map/scatter-add | solution.py:87
  146.8 5.8 %convolution_add_fusion.1 = f32[2048,1536]{1,0:T(8,128)S(1)} fusion(bf16[512,1536]{1,0:T(8,128)(2,1)} %param.31, f32[1536]{0:T(1024)S(1)} %get-tuple-element.24, f32[2048,512]{1,0:T(8,128)} %scatter_custom_fusion.4, f32[2048]{0:T(1024)S(1)} %broadcast_maximum_fusion), kind=kOutput, calls=%fused_computation.11 | convolution fusion | flops 3226468352 | bytes 18364416 | tf_op jit(solution)/shard_map/dot_general | solution.py:90
  152.6 8.6 %fusion.1 = bf16[2048,512]{1,0:T(8,128)(2,1)} fusion(bf16[2048,512]{1,0:T(8,128)(2,1)S(1)} %copy-done.2, f32[2048,1536]{1,0:T(8,128)} %convolution_add_fusion, f32[2048,1536]{1,0:T(8,128)S(1)} %convolution_add_fusion.1, pred[2048]{0:T(1024)(128)(4,1)S(1)} %broadcast_compare_fusion), kind=kLoop, calls=%fused_computation.16 | loop fusion | flops 17825792 | bytes 29362176 | tf_op jit(solution)/shard_map/convert_element_type | solution.py:96
  161.2 23.9 %all-to-all-done.3 = bf16[128,40,512]{2,1,0:T(8,128)(2,1)} async-done(((bf16[128,40,512]{2,1,0:T(8,128)(2,1)}), bf16[128,40,512]{2,1,0:T(8,128)(2,1)}, u32[]{:S(2)}, u32[]{:S(2)}) %all-to-all-start.3) | async-done | bytes 5242912 | tf_op jit(solution)/shard_map/all_to_all | solution.py:103
  185.1 11.6 %gather_fusion.3 = bf16[2560,512]{1,0:T(8,128)(2,1)} fusion(bf16[5120,512]{1,0:T(8,128)(2,1)} %bitcast.13, s32[3072]{0:T(1024)S(1)} %pad_clamp_fusion), kind=kCustom, calls=%fused_computation.3 | custom fusion | bytes 5253120 | tf_op jit(solution)/shard_map/jit(_take)/gather | solution.py:14
  196.8 7.8 %convolution_convert_fusion = bf16[2560,1024]{1,0:T(8,128)(2,1)} fusion(bf16[640,1024]{1,0:T(8,128)(2,1)S(1)} %copy-done.16, bf16[2560,128]{1,0:T(8,128)(2,1)S(1)} %copy-done.5, bf16[2560,512]{1,0:T(8,128)(2,1)} %gather_fusion.3), kind=kOutput, calls=%fused_computation.12 | convolution fusion | flops 3364618240 | bytes 9830400 | tf_op jit(solution)/shard_map/while/body/eval_jaxpr/dot_general | solution.py:121
  204.5 9.3 %reshape.419 = bf16[128,20,2,4,128]{4,3,2,1,0:T(4,128)(2,1)} reshape(bf16[2560,1024]{1,0:T(8,128)(2,1)} %convolution_convert_fusion) | data formatting | bytes 10485760 | tf_op jit(solution)/shard_map/while/body/eval_jaxpr/reshape | solution.py:123
  213.9 5.9 %slice_bitcast_fusion = (bf16[128,20,4,128]{3,2,1,0:T(4,128)(2,1)}, bf16[128,20,4,128]{3,2,1,0:T(4,128)(2,1)S(1)}) fusion(bf16[128,20,2,4,128]{4,3,2,1,0:T(4,128)(2,1)} %reshape.419), kind=kLoop, calls=%fused_computation.39 | loop fusion | bytes 10485760 | tf_op jit(solution)/shard_map/while/body/eval_jaxpr/squeeze | solution.py:133
  219.8 1.7 fusion.18
  221.9 2.9 %fusion.16 = f32[128,4,1,128]{3,2,1,0:T(1,128)S(1)} fusion(bf16[128,4,20,1]{2,3,1,0:T(2,128)(2,1)S(1)} %copy.69, bf16[128,20,4,128]{3,2,1,0:T(4,128)(2,1)} %get-tuple-element.40), kind=kOutput, calls=%fused_computation.35 | convolution fusion | flops 2621440 | bytes 2904064 | tf_op jit(solution)/shard_map/while/body/eval_jaxpr/ehk,ekhc->ehc/dot_general | solution.py:132
  (113 shorter events, 20.7 us)
Async XLA Ops:
  0.6 70.6 %copy-start = (bf16[1152,1024]{1,0:T(8,128)(2,1)S(1)}, bf16[1152,1024]{1,0:T(8,128)(2,1)}, u32[]{:S(2)}) copy-start(bf16[1152,1024]{1,0:T(8,128)(2,1)} %param.24) | copy-start | bytes 7077892
  5.3 22.1 %all-to-all-start = ((s32[128,1,4]{2,1,0:T(1,128)}), s32[128,1,4]{2,1,0:T(1,128)S(1)}, u32[]{:S(2)}, u32[]{:S(2)}) async-start(s32[128,1,4]{2,1,0:T(1,128)} %bitcast.5), calls=%async_computation | async-start | bytes 131072 | tf_op jit(solution)/shard_map/all_to_all | solution.py:54
  19.1 1.1 copy-start.3
  21.8 3.2 %copy-start.14 = (s32[128]{0:T(128)S(1)}, s32[128]{0:T(128)}, u32[]{:S(2)}) copy-start(s32[128]{0:T(128)} %param.19) | copy-start | bytes 1540
  34.0 24.9 %all-to-all-start.1 = ((bf16[128,4,512]{2,1,0:T(4,128)(2,1)}), bf16[128,4,512]{2,1,0:T(4,128)(2,1)S(1)}, u32[]{:S(2)}, u32[]{:S(2)}) async-start(bf16[128,4,512]{2,1,0:T(4,128)(2,1)} %reshape.410), calls=%async_computation.1 | async-start | bytes 1048576 | tf_op jit(solution)/shard_map/all_to_all | solution.py:56
  58.9 19.6 %all-to-all-start.2 = ((s32[128,1,40]{2,1,0:T(1,128)}), s32[128,1,40]{2,1,0:T(1,128)}, u32[]{:S(2)}, u32[]{:S(2)}) async-start(s32[128,1,40]{2,1,0:T(1,128)} %bitcast.11), calls=%async_computation.2 | async-start | bytes 131072 | tf_op jit(solution)/shard_map/all_to_all | solution.py:101
  69.2 2.0 copy-start.9
  69.2 2.0 copy-start.17
  69.3 2.0 copy-start.18
  74.1 14.5 %copy-start.2 = (bf16[2048,512]{1,0:T(8,128)(2,1)S(1)}, bf16[2048,512]{1,0:T(8,128)(2,1)}, u32[]{:S(2)}) copy-start(bf16[2048,512]{1,0:T(8,128)(2,1)} %param.17) | copy-start | bytes 6291460
  78.4 31.5 %all-to-all-start.4 = ((bf16[128,4,512]{2,1,0:T(4,128)(2,1)}), bf16[128,4,512]{2,1,0:T(4,128)(2,1)S(1)}, u32[]{:S(2)}, u32[]{:S(2)}) async-start(bf16[128,4,512]{2,1,0:T(4,128)(2,1)} %reshape.422), calls=%async_computation.4 | async-start | bytes 1048576 | tf_op jit(solution)/shard_map/all_to_all | solution.py:83
  109.9 0.8 copy-start.4
  109.9 11.0 %copy-start.11 = (s32[128,20]{0,1:T(8,128)S(1)}, s32[128,20]{0,1:T(8,128)}, u32[]{:S(2)}) copy-start(s32[128,20]{0,1:T(8,128)} %param.21) | copy-start | bytes 30724
  110.0 11.0 %copy-start.15 = (s32[128]{0:T(128)S(1)}, s32[128]{0:T(128)}, u32[]{:S(2)}) copy-start(s32[128]{0:T(128)} %param.19) | copy-start | bytes 1540
  110.0 11.2 %copy-start.10 = (f32[2,1536]{1,0:T(2,128)S(1)}, f32[2,1536]{1,0:T(2,128)}, u32[]{:S(2)}) copy-start(f32[2,1536]{1,0:T(2,128)} %param.33) | copy-start | bytes 36868
  110.0 11.2 %copy-start.12 = (f32[128]{0:T(128)S(1)}, f32[128]{0:T(128)}, u32[]{:S(2)}) copy-start(f32[128]{0:T(128)} %param.23) | copy-start | bytes 1540
  110.0 11.2 %copy-start.13 = (f32[128]{0:T(128)S(1)}, f32[128]{0:T(128)}, u32[]{:S(2)}) copy-start(f32[128]{0:T(128)} %param.22) | copy-start | bytes 1540
  110.7 74.4 %all-to-all-start.3 = ((bf16[128,40,512]{2,1,0:T(8,128)(2,1)}), bf16[128,40,512]{2,1,0:T(8,128)(2,1)}, u32[]{:S(2)}, u32[]{:S(2)}) async-start(bf16[128,40,512]{2,1,0:T(8,128)(2,1)} %bitcast.73), calls=%async_computation.3 | async-start | bytes 10485760 | tf_op jit(solution)/shard_map/all_to_all | solution.py:103
  126.9 11.8 %copy-start.6 = (bf16[512,512]{1,0:T(8,128)(2,1)S(1)}, bf16[512,512]{1,0:T(8,128)(2,1)}, u32[]{:S(2)}) copy-start(bf16[512,512]{1,0:T(8,128)(2,1)} %param.28) | copy-start | bytes 1572868
  185.1 11.6 %copy-start.5 = (bf16[2560,128]{1,0:T(8,128)(2,1)S(1)}, bf16[2560,128]{1,0:T(8,128)(2,1)}, u32[]{:S(2)}) copy-start(bf16[2560,128]{1,0:T(8,128)(2,1)} %cosine_convert_fusion) | copy-start | bytes 1966084
  185.1 11.6 %copy-start.16 = (bf16[640,1024]{1,0:T(8,128)(2,1)S(1)}, bf16[640,1024]{1,0:T(8,128)(2,1)}, u32[]{:S(2)}) copy-start(bf16[640,1024]{1,0:T(8,128)(2,1)} %param.29) | copy-start | bytes 3932164
  213.9 5.9 %copy-start.8 = (bf16[128,4,128,1]{2,3,1,0:T(2,128)(2,1)S(1)}, bf16[128,4,128,1]{2,3,1,0:T(2,128)(2,1)}, u32[]{:S(2)}) copy-start(bf16[128,4,128,1]{2,3,1,0:T(2,128)(2,1)} %reshape.515) | copy-start | bytes 393220
  221.5 3.5 %copy-start.7 = (bf16[512,512]{1,0:T(8,128)(2,1)S(1)}, bf16[512,512]{1,0:T(8,128)(2,1)}, u32[]{:S(2)}) copy-start(bf16[512,512]{1,0:T(8,128)(2,1)} %param.30) | copy-start | bytes 1572868
  221.7 4.1 %copy-start.1 = (bf16[1152,1024]{1,0:T(8,128)(2,1)S(1)}, bf16[1152,1024]{1,0:T(8,128)(2,1)}, u32[]{:S(2)}) copy-start(bf16[1152,1024]{1,0:T(8,128)(2,1)} %param.24) | copy-start | bytes 7077892
where the time goes:
time: 227 us; the launch traced here: 226 us
  local copies, waits for them, and re-layouts  82.2 us (36%)
  starting transfers between devices  49.9 us (22%)
  other arithmetic  37.6 us (17%)
  matrix products  29.5 us (13%)
  waiting for transfers between devices  25.4 us (11%)
    gather x5, local copies, waits for them, and re-layouts, take_rows(): flat = jnp.take(table, indices.reshape(-1), axis=0, mode='clip')  40.2 us
    all_to_all x2, waiting for transfers between devices, on_device(): lax.all_to_all(rows, ('grp', 'dev'), split_axis=0, concat_axis=0, tiled=T...  23.9 us
    all_to_all x2, starting transfers between devices, on_device(): lax.all_to_all(rows, ('grp', 'dev'), split_axis=0, concat_axis=0, tiled=T...  19.9 us
    scatter x2, local copies, waits for them, and re-layouts, placing(): jnp.full((owners * capacity,), -1, jnp.int32).at[position].set(local_rows)  11.5 us
    all_to_all x1, starting transfers between devices, on_device(): lax.all_to_all(event_req, ('grp', 'dev'), split_axis=0, concat_axis=0, ti...  11.5 us
    all_to_all x1, starting transfers between devices, on_device(): lax.all_to_all(near_req, ('grp', 'dev'), split_axis=0, concat_axis=0, til...  10.2 us
    reshape x1, local copies, waits for them, and re-layouts, embed_block(): keyval = jnp.dot(feats, w_keyval, preferred_element_type=jnp.float32).ast...  9.35 us
    convert_element_type x1, other arithmetic, on_device(): jnp.where(counts[:, None] > 0.0, fresh, memory.astype(jnp.float32))  8.64 us
  transfers between devices with their start and end apart: 5, of which 2 were waited for; matrix products, arithmetic and copies ran while one was open for 42% of the time, Pallas kernels for 0%

commit v1 on v0

v1 whole, which is shorter than its diff:
```python
import functools

import jax
import jax.numpy as jnp
from jax import lax
from jax.experimental import pallas as pl
from jax.experimental.pallas import tpu as pltpu
from jax.sharding import PartitionSpec as P

HDIM = 128
LANES = 128
AXES = ("grp", "dev")
F32 = jnp.float32
BF16 = jnp.bfloat16
NEG = -1e30
NT = (((1,), (1,)), ((), ()))


def dotf(a, b):
    return jnp.dot(a, b, preferred_element_type=F32)


def exchange(x):
    return lax.all_to_all(x, AXES, split_axis=0, concat_axis=0, tiled=True)


def call(kernel, out_shape, *args, scalars=0, scratch=(), mib=16):
    return pl.pallas_call(
        kernel,
        out_shape=out_shape,
        grid_spec=pltpu.PrefetchScalarGridSpec(
            num_scalar_prefetch=scalars,
            grid=(),
            in_specs=[pl.BlockSpec(memory_space=pltpu.VMEM)] * (len(args) - scalars),
            out_specs=jax.tree.map(lambda _: pl.BlockSpec(memory_space=pltpu.VMEM), out_shape),
            scratch_shapes=scratch,
        ),
        compiler_params=pltpu.CompilerParams(vmem_limit_bytes=mib << 20),
    )(*args)


def hbm(x):
    return pltpu.with_memory_space_constraint(x, pltpu.HBM)


def vmem(x):
    return pltpu.with_memory_space_constraint(x, pltpu.VMEM)


def whole(x):
    zeros = (0,) * x.ndim
    return pl.BlockSpec(x.shape, lambda *_: zeros)


def sds(shape, dtype):
    return jax.ShapeDtypeStruct(shape, dtype)


def place_kernel(shift, cap_n, cap_e, rows, nid_ref, nt_ref, en_ref, tick_ref, req_ref, map_ref, dt_ref):
    fanout, events = nid_ref.shape
    owners = req_ref.shape[0]
    i0 = lax.broadcasted_iota(jnp.int32, (owners, events), 0)
    e0 = lax.broadcasted_iota(jnp.int32, (events, events), 0)
    e1 = lax.broadcasted_iota(jnp.int32, (events, events), 1)
    tri = jnp.where(e0 <= e1, 1.0, 0.0)
    both = jnp.concatenate([tri, jnp.ones((events, events), F32)], axis=1).astype(BF16)
    srow = lax.broadcasted_iota(jnp.int32, (rows, events), 0)
    lane = lax.broadcasted_iota(jnp.int32, (1, events), 1)
    tick = tick_ref[...]
    mask = (1 << shift) - 1
    acc = jnp.zeros((6 * rows, owners), F32)
    base = jnp.zeros((owners, events), F32)
    zero = jnp.zeros((1, events), jnp.int32)
    for k in range(fanout + 2):
        near = k < fanout
        if k == fanout:
            base = jnp.zeros((owners, events), F32)
        ids = nid_ref[k : k + 1, :] if near else en_ref[k - fanout : k - fanout + 1, :]
        local = jnp.bitwise_and(ids, mask)
        hit = i0 == jnp.right_shift(ids, shift)
        onehot = jnp.where(hit, 1.0, 0.0)
        ohb = onehot.astype(BF16)
        ranks = dotf(ohb, both)
        cum = ranks[:, :events] + base
        base = base + ranks[:, events:]
        slot = jnp.sum(onehot * cum, axis=0, keepdims=True).astype(jnp.int32) - 1
        if near:
            d = tick - nt_ref[k : k + 1, :] + 131072
            code = lane + 1
            parts = (d & 255, jnp.right_shift(d, 8) & 255, jnp.right_shift(d, 16))
            value = local
        else:
            slot = slot + cap_n
            code = lane + (1 + events * (k - fanout))
            parts = (zero, zero, zero)
            value = local + 1
        vals = (value & 255, jnp.right_shift(value, 8), code) + parts
        so = srow == slot
        table = jnp.concatenate([jnp.where(so, v.astype(F32), 0.0) for v in vals], axis=0)
        acc = acc + lax.dot_general(table.astype(BF16), ohb, NT, preferred_element_type=F32)
    a = [acc[i * rows : (i + 1) * rows] for i in range(6)]
    pad = jnp.zeros((LANES - rows, owners), F32)

    def turned(x):
        return jnp.concatenate([x, pad], axis=0).T

    req_ref[...] = turned(a[0] + 256.0 * a[1]).astype(jnp.int32)
    map_ref[...] = turned(a[2]).astype(jnp.int32)
    dt = a[3] + 256.0 * a[4] + 65536.0 * a[5] - 131072.0
    dt_ref[...] = turned(jnp.where(a[2] > 0.0, dt, 0.0))


def spread_kernel(mem_ref, out_ref):
    nodes, width = mem_ref.shape
    parts = width // LANES
    block = 128

    def step(i, carry):
        r = pl.multiple_of(i * block, block)
        for c in range(parts):
            part = mem_ref[pl.ds(r, block), c * LANES : (c + 1) * LANES].astype(F32)
            out_ref[pl.ds(r * parts + c, block, stride=parts), :] = part
        return carry

    lax.fori_loop(0, nodes // block, step, 0)


def pick_kernel(cols, shifted, req_ref, mem_ref, out_ref, stage_ref):
    n = len(cols)
    parts = stage_ref.shape[0] // 32
    group = 16 // n if n < 16 else 1
    total = n * group
    steps = out_ref.shape[0] // total
    start = pl.program_id(0) * (out_ref.shape[0] // n)

    def step(i, carry):
        for g in range(group):
            o = start + i * group + g
            for j, col in enumerate(cols):
                row = req_ref[o, col]
                if shifted[j]:
                    row = jnp.maximum(row - 1, 0)
                at = pl.multiple_of(row * parts, parts)
                s = (g * n + j) * parts
                stage_ref[s : s + parts, :] = mem_ref[pl.ds(at, parts), :]
        r = pl.multiple_of(i * total, total)
        for c in range(parts):
            part = stage_ref[pl.ds(c, total, stride=parts), :]
            out_ref[pl.ds(r, total), c * LANES : (c + 1) * LANES] = part.astype(BF16)
        return carry

    lax.fori_loop(0, steps, step, 0)


def pick(req, mem32, width, cols, shifted):
    peers = req.shape[0]
    parts = width // LANES
    rows = peers * len(cols)
    blocks = 4
    return pl.pallas_call(
        functools.partial(pick_kernel, cols, shifted),
        out_shape=pltpu.HBM((rows, width), BF16),
        grid_spec=pltpu.PrefetchScalarGridSpec(
            num_scalar_prefetch=1,
            grid=(blocks,),
            in_specs=[pl.BlockSpec(memory_space=pltpu.VMEM)],
            out_specs=pl.BlockSpec((rows // blocks, width), lambda i, _: (i, 0)),
            scratch_shapes=[pltpu.VMEM((32 * parts, LANES), F32)],
        ),
        compiler_params=pltpu.CompilerParams(vmem_limit_bytes=8 << 20),
    )(hbm(req), vmem(mem32))


def message_kernel(cap_e, rows_ref, base_ref, code_ref, enc_ref, w1_ref, b1_ref, w2_ref, b2_ref, wq_ref, out_ref, q_ref):
    peers, per, width = rows_ref.shape
    slots = peers * per
    events = enc_ref.shape[0]
    code = code_ref[...]
    target = lax.broadcasted_iota(jnp.int32, (2 * events, slots), 0) + 1
    sel = jnp.where(target == code, 1.0, 0.0)
    rows = rows_ref[...].reshape(slots, width)
    pair = dotf(sel.astype(BF16), rows).astype(BF16)
    q_ref[...] = dotf(pair[:events], wq_ref[...]).astype(BF16)
    first = dotf(pair, w1_ref[:width, :])
    second = dotf(pair, w1_ref[width : 2 * width, :])
    third = dotf(enc_ref[...], w1_ref[2 * width :, :])
    both = jnp.concatenate([second[events:] + third, second[:events] + third], axis=0)
    hidden = jnp.maximum(first + both + b1_ref[...], 0.0).astype(BF16)
    msg = (dotf(hidden, w2_ref[...]) + b2_ref[...]).astype(BF16)
    placed = dotf(sel.T.astype(BF16), msg)
    j = lax.broadcasted_iota(jnp.int32, (slots, width), 0) & (per - 1)
    base = base_ref[...].reshape(slots, width).astype(F32)
    out = jnp.where(j < cap_e, placed, base).astype(BF16)
    out_ref[...] = out.reshape(peers, per, width)


def messages(cap_e, got, base, code, enc, *weights):
    peers, _, width = got.shape
    tile = pl.BlockSpec((peers, 8, width), lambda i: (0, 0, 0))
    args = (hbm(got), hbm(base), code, enc, *weights)
    q_shape = sds((enc.shape[0], width), BF16)
    return pl.pallas_call(
        functools.partial(message_kernel, cap_e),
        out_shape=(pltpu.HBM(base.shape, BF16), q_shape),
        grid=(1,),
        in_specs=[tile, tile] + [whole(x) for x in args[2:]],
        out_specs=(tile, whole(q_shape)),
        input_output_aliases={1: 0},
        compiler_params=pltpu.CompilerParams(vmem_limit_bytes=24 << 20),
    )(*args)


def gru_kernel(msgs_ref, old_ref, gh_ref, to_c_ref, to_t_ref, mem_ref, wi_ref, bias_ref, out_ref, fresh_ref, lead_ref):
    peers, per, width = msgs_ref.shape
    slots = old_ref.shape[0]
    block = mem_ref.shape[0]
    step = pl.program_id(0)

    @pl.when(step == 0)
    def _():
        row = to_c_ref[...].astype(F32)
        col = jnp.broadcast_to(row, (8, slots)).T[:, 0:1]
        tiles = to_t_ref[...].astype(F32)
        hits = jnp.where(jnp.logical_and(col == tiles, tiles > 0.0), 1.0, 0.0)
        counts = jnp.sum(hits, axis=1, keepdims=True)
        sums = dotf(hits.astype(BF16), msgs_ref[...].reshape(peers * per, width))
        mean = (sums / jnp.maximum(counts, 1.0)).astype(BF16)
        s0 = lax.broadcasted_iota(jnp.int32, (slots, slots), 0)
        s1 = lax.broadcasted_iota(jnp.int32, (slots, slots), 1)
        same = jnp.logical_and(col == row, s0 < s1)
        earlier = jnp.max(jnp.where(same, 1.0, 0.0), axis=0, keepdims=True)
        lead_ref[...] = jnp.where(earlier > 0.0, 0.0, row)
        old = old_ref[...].astype(F32)
        gi = dotf(mean, wi_ref[...]) + bias_ref[0:1, :]
        gh = gh_ref[...]
        r = jax.nn.sigmoid(gi[:, :width] + gh[:, :width])
        z = jax.nn.sigmoid(gi[:, width : 2 * width] + gh[:, width : 2 * width])
        c = jnp.tanh(gi[:, 2 * width :] + r * gh[:, 2 * width :])
        fresh_ref[...] = ((1.0 - z) * c + z * old).astype(BF16)

    node = lax.broadcasted_iota(jnp.int32, (block, slots), 0) + (step * block + 1)
    hit = jnp.where(node.astype(F32) == lead_ref[...], 1.0, 0.0)
    reached = jnp.max(hit, axis=1, keepdims=True)
    new = dotf(hit.astype(BF16), fresh_ref[...])
    out_ref[...] = jnp.where(reached > 0.0, new, mem_ref[...].astype(F32)).astype(BF16)


def update(got, old, gh, to_c, to_t, memory, wi, bias):
    peers, _, width = got.shape
    nodes = memory.shape[0]
    slots = old.shape[0]
    block = 512
    tile = pl.BlockSpec((peers, 8, width), lambda i: (0, 0, 0))
    part = pl.BlockSpec((block, width), lambda i: (i, 0))
    return pl.pallas_call(
        gru_kernel,
        out_shape=sds(memory.shape, BF16),
        grid=(nodes // block,),
        in_specs=[tile] + [whole(x) for x in (old, gh, to_c, to_t)] + [part, whole(wi), whole(bias)],
        out_specs=part,
        scratch_shapes=[pltpu.VMEM((slots, width), BF16), pltpu.VMEM((1, slots), F32)],
        compiler_params=pltpu.CompilerParams(vmem_limit_bytes=28 << 20),
    )(hbm(got), hbm(old), hbm(gh), to_c, to_t, hbm(memory), wi, bias)


def attend_kernel(first, last, *refs):
    rows_ref, enc_ref, map_ref, q_ref, w_ref = refs[:5]
    at = 5
    if not first:
        start = refs[at : at + 3]
        at += 3
    if last:
        wo_ref, out_ref, m_ref, l_ref, a_ref = refs[at:]
    else:
        m_ref, l_ref, a_ref = refs[at:]
    step = pl.program_id(0)
    slots, width = rows_ref.shape
    events = q_ref.shape[0]
    heads = width // HDIM

    @pl.when(step == 0)
    def _():
        if first:
            m_ref[...] = jnp.full((events, width), NEG, F32)
            l_ref[...] = jnp.zeros((events, width), F32)
            a_ref[...] = jnp.zeros((events, width), F32)
        else:
            for dst, src in zip((m_ref, l_ref, a_ref), start):
                dst[...] = src[...]

    kv = dotf(rows_ref[...], w_ref[:width, :]) + dotf(enc_ref[...], w_ref[width:, :])
    kv = kv.astype(BF16)
    event = lax.broadcasted_iota(jnp.int32, (events, slots), 0) + 1
    mine = event == map_ref[...]
    for h in range(heads):
        cut = slice(h * HDIM, (h + 1) * HDIM)
        s = lax.dot_general(q_ref[:, cut], kv[:, cut], NT, preferred_element_type=F32)
        s = jnp.where(mine, s * (1.0 / HDIM**0.5), NEG)
        m_old = m_ref[:, cut]
        m = jnp.maximum(m_old, jnp.max(s, axis=1, keepdims=True))
        p = jnp.where(mine, jnp.exp(s - m[:, 0:1]), 0.0)
        scale = jnp.exp(m_old - m)
        m_ref[:, cut] = m
        l_ref[:, cut] = scale * l_ref[:, cut] + jnp.sum(p, axis=1, keepdims=True)
        add = dotf(p.astype(BF16), kv[:, width + h * HDIM : width + (h + 1) * HDIM])
        a_ref[:, cut] = scale * a_ref[:, cut] + add

    if last:

        @pl.when(step == pl.num_programs(0) - 1)
        def _():
            attn = (a_ref[...] / l_ref[...]).astype(BF16)
            out_ref[...] = dotf(attn, wo_ref[...]).astype(BF16)


def attend(rows, enc, slot_map, query, w, state=None, w_out=None):
    first, last = state is None, w_out is not None
    total, width = rows.shape
    events = query.shape[0]
    block = 1024
    shapes = tuple(pltpu.VMEM((events, width), F32) for _ in range(3))
    kept = tuple(vmem(x) for x in state) if state else ()
    args = (hbm(rows), hbm(enc), slot_map, query, w) + kept + ((w_out,) if last else ())
    in_specs = [
        pl.BlockSpec((block, width), lambda i: (i, 0)),
        pl.BlockSpec((block, LANES), lambda i: (i, 0)),
        pl.BlockSpec((1, block), lambda i: (0, i)),
    ] + [whole(x) for x in args[3:]]
    final = sds((events, width), BF16)
    return pl.pallas_call(
        functools.partial(attend_kernel, first, last),
        out_shape=final if last else shapes,
        grid=(total // block,),
        in_specs=in_specs,
        out_specs=whole(final) if last else tuple(whole(final) for _ in shapes),
        scratch_shapes=[pltpu.VMEM((events, width), F32)] * 3 if last else [],
        compiler_params=pltpu.CompilerParams(vmem_limit_bytes=24 << 20),
    )(*args)


def encode(dt, freq, phase):
    return jnp.cos(dt[..., None] * freq + phase).astype(BF16)


def on_device(
    memory,
    event_nodes,
    event_ticks,
    neighbour_ids,
    neighbour_ticks,
    freq,
    phase,
    w_msg1,
    b_msg1,
    w_msg2,
    b_msg2,
    w_query,
    w_keyval,
    w_out,
    gru_input,
    gru_hidden,
    gru_bias,
):
    owners = lax.axis_size(AXES)
    nodes, width = memory.shape
    events, fanout = neighbour_ids.shape
    cap_e = 4 * events // owners
    cap_n = 2 * fanout * events // owners
    rows = cap_n + 8
    shift = nodes.bit_length() - 1
    assert nodes == 1 << shift and cap_e == 4 and cap_n == 40
    table = (owners, LANES)
    req, owner_map, dt = call(
        functools.partial(place_kernel, shift, cap_n, cap_e, rows),
        (sds(table, jnp.int32), sds(table, jnp.int32), sds(table, F32)),
        hbm(neighbour_ids.T),
        hbm(neighbour_ticks.T),
        hbm(event_nodes.T),
        hbm(event_ticks.reshape(1, events)),
        mib=8,
    )
    mem32 = call(spread_kernel, pltpu.VMEM((nodes * width // LANES, LANES), F32), hbm(memory), mib=8)
    asked = exchange(req)

    half = 8 - cap_e
    near = 28
    ev = tuple(range(cap_n, cap_n + cap_e))
    cols_a = ev + tuple(range(near))
    cols_c = tuple(range(near, near + cap_e)) + tuple(range(near, cap_n))
    take = functools.partial(pick, asked, mem32, width)
    sent_a = take(cols_a, (True,) * cap_e + (False,) * near)
    got_a = exchange(sent_a)
    base_c = take(cols_c, (False,) * len(cols_c)).reshape(owners, -1, width)
    old = take(ev, (True,) * cap_e)

    def spaced(x, width):
        return jnp.concatenate([jnp.zeros((owners, width), x.dtype), x], axis=1)

    def tiled(x):
        return jnp.concatenate([x, jnp.zeros((owners, half), x.dtype)], axis=1).reshape(1, -1)

    code = tiled(owner_map[:, cap_n : cap_n + cap_e])
    map_a = spaced(owner_map[:, :near], cap_e).reshape(1, -1)
    map_c = spaced(owner_map[:, near:cap_n], cap_e).reshape(1, -1)
    to = asked[:, cap_n : cap_n + cap_e]
    to_t = tiled(to)
    to_c = to.reshape(1, -1)
    gh = jnp.dot(old, gru_hidden, preferred_element_type=F32) + gru_bias[1]
    enc_a = encode(spaced(dt[:, :near], cap_e), freq, phase).reshape(-1, LANES)
    enc_c = encode(spaced(dt[:, near:cap_n], cap_e), freq, phase).reshape(-1, LANES)
    enc = encode(event_ticks.astype(F32), freq, phase)
    got_a, enc_a, enc_c, map_a, map_c, gh, old, to_c, to_t = lax.optimization_barrier(
        (got_a, enc_a, enc_c, map_a, map_c, gh, old, to_c, to_t)
    )
    sent_c, query = messages(
        cap_e,
        got_a.reshape(owners, -1, width),
        base_c,
        code,
        enc,
        w_msg1,
        b_msg1.reshape(1, -1),
        w_msg2,
        b_msg2.reshape(1, -1),
        w_query,
    )
    got_c = exchange(sent_c)
    state = attend(got_a, enc_a, map_a, query, w_keyval)
    new_memory = update(got_c, old, gh, to_c, to_t, memory, gru_input, gru_bias)
    embedding = attend(got_c.reshape(-1, width), enc_c, map_c, query, w_keyval, state, w_out)
    return (embedding, new_memory)


def solution(mesh):
    split = P(AXES, None)
    in_specs = (split, split, P(AXES), split, split) + (P(),) * 12
    return jax.shard_map(
        on_device, mesh=mesh, in_specs=in_specs, out_specs=(split, split), check_vma=False
    )
```

time: 227 us -> 158 us (0.70)
  local copies, waits for them, and re-layouts: 82.2 us -> 15.3 us
  Pallas kernels: 0 us -> 62 us
  starting transfers between devices: 49.9 us -> 23.1 us
  matrix products: 29.5 us -> 3.79 us
  other arithmetic: 37.6 us -> 13.7 us
  waiting for transfers between devices: 25.4 us -> 38.2 us
    pallas_call x0 -> x9, Pallas kernels: none -> 62 us  [the longest x2 25.6 us: attend(): pl.pallas_call(functools.partial(attend_kernel, first, last), out_shape=f...]
    gather x5 -> x0, local copies, waits for them, and re-layouts: 40.2 us -> none  [take_rows(): flat = jnp.take(table, indices.reshape(-1), axis=0, mode='clip')]
    all_to_all x5 -> x3, starting transfers between devices: 49.9 us -> 23.1 us  [exchange(): return lax.all_to_all(x, AXES, split_axis=0, concat_axis=0, tiled=True)]
    dot_general x8 -> x1, matrix products: 29.5 us -> 3.79 us  [on_device(): gh = jnp.dot(old, gru_hidden, preferred_element_type=F32) + gru_bias[1]]
    scatter x3 -> x0, local copies, waits for them, and re-layouts: 13.4 us -> none  [the longest x2 11.5 us: placing(): jnp.full((owners * capacity,), -1, jnp.int32).at[position].set(local_rows)]
    all_to_all x5 -> x3, waiting for transfers between devices: 25.4 us -> 38.2 us  [exchange(): return lax.all_to_all(x, AXES, split_axis=0, concat_axis=0, tiled=True)]
    reshape x12 -> x5, local copies, waits for them, and re-layouts: 12.8 us -> 2.3 us  [the longest x2 0.78 us: tiled(): jnp.concatenate([x, jnp.zeros((owners, half), x.dtype)], axis=1)]
    scatter-add x2 -> x0, other arithmetic: 9.43 us -> none  [the longest x1 5.97 us: on_device(): sums = jnp.zeros((node_dev, width), jnp.float32).at[target].add(terms)]
  transfers between devices with their start and end apart: 5 -> 3, of which waited for: 2 -> 3; matrix products, arithmetic and copies ran while one was open for 42% -> 13% of each run, Pallas kernels for 0% -> 18%
where the time goes in v1:
time: 158 us; the launch traced here: 157 us
  Pallas kernels  62 us (39%)
  waiting for transfers between devices  38.2 us (24%)
  starting transfers between devices  23.1 us (15%)
  local copies, waits for them, and re-layouts  15.3 us (10%)
  other arithmetic  13.7 us (9%)
  matrix products  3.79 us (2%)
    all_to_all x3, waiting for transfers between devices, exchange(): return lax.all_to_all(x, AXES, split_axis=0, concat_axis=0, tiled=True)  38.2 us
    pallas_call x2, Pallas kernels, attend(): pl.pallas_call(functools.partial(attend_kernel, first, last), out_shape=f...  25.6 us
    all_to_all x3, starting transfers between devices, exchange(): return lax.all_to_all(x, AXES, split_axis=0, concat_axis=0, tiled=True)  23.1 us
    pallas_call x3, Pallas kernels, pick(): pl.pallas_call(functools.partial(pick_kernel, cols, shifted), out_shape=p...  18.9 us
    convert_element_type x3, other arithmetic, encode(): return jnp.cos(dt[..., None] * freq + phase).astype(BF16)  13.6 us
    unnamed x48, local copies, waits for them, and re-layouts  12.1 us
    pallas_call x1, Pallas kernels, update(): pl.pallas_call(gru_kernel, out_shape=sds(memory.shape, BF16), grid=(nodes...  8.22 us
    pallas_call x2, Pallas kernels, call(): pl.pallas_call(kernel, out_shape=out_shape, grid_spec=pltpu.PrefetchScala...  4.86 us
  transfers between devices with their start and end apart: 3, of which 3 were waited for; matrix products, arithmetic and copies ran while one was open for 13% of the time, Pallas kernels for 18%

profile of v1, /device:TPU:1, one launch (start us, length us, event | category | flops | bytes accessed | tf_op | source)
XLA Modules:
  0.0 156.9 jit_solution(9851782325179991048)
XLA Ops:
  0.6 2.9 %shard_map.176 = (s32[128,128]{1,0:T(8,128)}, s32[128,128]{1,0:T(8,128)S(1)}, f32[128,128]{1,0:T(8,128)S(1)}) custom-call(s32[20,128]{1,0:T(8,128)} %bitcast.29, s32[20,128]{1,0:T(8,128)} %bitcast.30, s32[2,128]{1,0:T(2,128)} %bitcast.31, s32[1,128]{1,0:T(1,128)} %bitcast.32), custom_call_target="tpu_custom_call" | custom-call | tf_op jit(solution)/shard_map/pallas_call | solution.py:28
  3.5 11.5 %all-to-all-start = ((s32[128,1,128]{2,1,0:T(1,128)}), s32[128,1,128]{2,1,0:T(1,128)S(1)}, u32[]{:S(2)}, u32[]{:S(2)}) async-start(s32[128,1,128]{2,1,0:T(1,128)} %bitcast.5), calls=%async_computation | async-start | bytes 131072 | tf_op jit(solution)/shard_map/all_to_all | solution.py:24
  15.0 2.0 %shard_map.177.mem_ref = f32[8192,128]{1,0:T(8,128)S(1)} custom-call(bf16[2048,512]{1,0:T(8,128)(2,1)} %mem_ref.3), custom_call_target="tpu_custom_call" | custom-call | tf_op jit(solution)/shard_map/pallas_call | solution.py:28
  17.0 2.0 %copy-done.1 = f32[8192,128]{1,0:T(8,128)} copy-done((f32[8192,128]{1,0:T(8,128)}, f32[8192,128]{1,0:T(8,128)S(1)}, u32[]{:S(2)}) %copy-start.1) | copy-done | bytes 4194328
  19.0 5.4 %all-to-all-done = s32[128,1,128]{2,1,0:T(1,128)S(1)} async-done(((s32[128,1,128]{2,1,0:T(1,128)}), s32[128,1,128]{2,1,0:T(1,128)S(1)}, u32[]{:S(2)}, u32[]{:S(2)}) %all-to-all-start) | async-done | bytes 65568 | tf_op jit(solution)/shard_map/all_to_all | solution.py:24
  24.4 0.6 copy-done.19
  25.1 2.2 %copy-done.2 = f32[8192,128]{1,0:T(8,128)S(1)} copy-done((f32[8192,128]{1,0:T(8,128)S(1)}, f32[8192,128]{1,0:T(8,128)}, u32[]{:S(2)}) %copy-start.2) | copy-done | bytes 4194328
  27.3 8.8 %shard_map.178 = bf16[4096,512]{1,0:T(8,128)(2,1)} custom-call(s32[128,128]{1,0:T(8,128)} %bitcast.25, f32[8192,128]{1,0:T(8,128)S(1)} %copy-done.2), custom_call_target="tpu_custom_call" | custom-call | tf_op jit(solution)/shard_map/pallas_call | solution.py:160
  36.1 5.6 %all-to-all-start.1 = ((bf16[128,32,512]{2,1,0:T(8,128)(2,1)}), bf16[128,32,512]{2,1,0:T(8,128)(2,1)}, u32[]{:S(2)}, u32[]{:S(2)}) async-start(bf16[128,32,512]{2,1,0:T(8,128)(2,1)} %bitcast.24), calls=%async_computation.1 | async-start | bytes 8388608 | tf_op jit(solution)/shard_map/all_to_all | solution.py:24
  42.0 0.1 reshape.55.refs_2_
  42.6 0.7 reshape.56.refs_2_
  43.5 0.3 cosine_convert_fusion.2.enc_ref
  43.8 4.7 %cosine_convert_fusion.1.refs_1_ = bf16[2048,128]{1,0:T(8,128)(2,1)} fusion(f32[128]{0:T(128)S(1)} %copy-done.21, f32[128]{0:T(128)S(1)} %copy-done.22, f32[2048]{0:T(1024)S(1)} %mul.49), kind=kLoop, calls=%fused_computation.2 | loop fusion | flops 786432 | bytes 533504 | tf_op jit(solution)/shard_map/convert_element_type | solution.py:342
  48.5 8.7 %cosine_convert_fusion.refs_1_ = bf16[4096,128]{1,0:T(8,128)(2,1)} fusion(f32[128]{0:T(128)S(1)} %copy-done.21, f32[128]{0:T(128)S(1)} %copy-done.22, f32[4096]{0:T(1024)S(1)} %mul.45), kind=kLoop, calls=%fused_computation.1 | loop fusion | flops 1572864 | bytes 1065984 | tf_op jit(solution)/shard_map/convert_element_type | solution.py:342
  57.2 0.7 reshape.57.to_c_ref
  57.9 2.2 %copy-done.3 = f32[8192,128]{1,0:T(8,128)S(1)} copy-done((f32[8192,128]{1,0:T(8,128)S(1)}, f32[8192,128]{1,0:T(8,128)}, u32[]{:S(2)}) %copy-start.3) | copy-done | bytes 4194328
  60.1 4.0 %shard_map.179.old_ref = bf16[512,512]{1,0:T(8,128)(2,1)} custom-call(s32[128,128]{1,0:T(8,128)} %bitcast.26, f32[8192,128]{1,0:T(8,128)S(1)} %copy-done.3), custom_call_target="tpu_custom_call" | custom-call | tf_op jit(solution)/shard_map/pallas_call | solution.py:160
  64.2 6.1 %shard_map.180 = bf16[2048,512]{1,0:T(8,128)(2,1)} custom-call(s32[128,128]{1,0:T(8,128)} %bitcast.27, f32[8192,128]{1,0:T(8,128)S(1)} %copy-done.3), custom_call_target="tpu_custom_call" | custom-call | tf_op jit(solution)/shard_map/pallas_call | solution.py:160
  70.2 0.7 reshape.58.to_t_ref
  70.9 3.8 %convolution_add_fusion.gh_ref = f32[512,1536]{1,0:T(8,128)} fusion(bf16[512,512]{1,0:T(8,128)(2,1)} %shard_map.179.old_ref, bf16[512,1536]{1,0:T(8,128)(2,1)S(1)} %copy-done, f32[1536]{0:T(1024)S(1)} %slice_reduce_fusion), kind=kOutput, calls=%fused_computation | convolution fusion | flops 806092800 | bytes 5249024 | tf_op jit(solution)/shard_map/dot_general | solution.py:408
  74.7 19.6 %all-to-all-done.1 = bf16[128,32,512]{2,1,0:T(8,128)(2,1)} async-done(((bf16[128,32,512]{2,1,0:T(8,128)(2,1)}), bf16[128,32,512]{2,1,0:T(8,128)(2,1)}, u32[]{:S(2)}, u32[]{:S(2)}) %all-to-all-start.1) | async-done | bytes 4194336 | tf_op jit(solution)/shard_map/all_to_all | solution.py:24
  94.4 1.7 %copy-done.5 = bf16[1152,1024]{1,0:T(8,128)(2,1)S(1)} copy-done((bf16[1152,1024]{1,0:T(8,128)(2,1)S(1)}, bf16[1152,1024]{1,0:T(8,128)(2,1)}, u32[]{:S(2)}) %copy-start.5) | copy-done | bytes 2359320
  96.0 4.4 %shard_map.181 = (bf16[128,16,512]{2,1,0:T(8,128)(2,1)}, bf16[128,512]{1,0:T(8,128)(2,1)S(1)}) custom-call(bf16[128,32,512]{2,1,0:T(8,128)(2,1)} %bitcast.9.rows_ref, bf16[128,16,512]{2,1,0:T(8,128)(2,1)} %bitcast.23, s32[1,1024]{1,0:T(1,128)S(1)} %reshape.61.code_ref, ...), custom_call_target="tpu_custom_call", output_to_operand_aliasing={{0}: (1, {})} | custom-call | tf_op jit(solution)/shard_map/pallas_call | solution.py:202
  100.4 6.0 %all-to-all-start.2 = ((bf16[128,16,512]{2,1,0:T(8,128)(2,1)}), bf16[128,16,512]{2,1,0:T(8,128)(2,1)}, u32[]{:S(2)}, u32[]{:S(2)}) async-start(bf16[128,16,512]{2,1,0:T(8,128)(2,1)} %get-tuple-element.23), calls=%async_computation.2 | async-start | bytes 4194304 | tf_op jit(solution)/shard_map/all_to_all | solution.py:24
  106.5 15.9 %shard_map.182 = (f32[128,512]{1,0:T(8,128)S(1)}, f32[128,512]{1,0:T(8,128)S(1)}, f32[128,512]{1,0:T(8,128)S(1)}) custom-call(bf16[4096,512]{1,0:T(8,128)(2,1)} %bitcast.8.refs_0_, bf16[4096,128]{1,0:T(8,128)(2,1)} %cosine_convert_fusion.refs_1_, s32[1,4096]{1,0:T(1,128)S(1)} %reshape.55.refs_2_, bf16[128,512]{1,0:T(8,128)(2,1)S(1)} %get-tuple-element.26.refs_3_, ...), custom_call_target="tpu_custom_call" | custom-call | tf_op jit(solution)/shard_map/pallas_call | solution.py:330
  122.4 0.7 copy-done.10
  123.1 13.2 %all-to-all-done.2.msgs_ref = bf16[128,16,512]{2,1,0:T(8,128)(2,1)} async-done(((bf16[128,16,512]{2,1,0:T(8,128)(2,1)}), bf16[128,16,512]{2,1,0:T(8,128)(2,1)}, u32[]{:S(2)}, u32[]{:S(2)}) %all-to-all-start.2) | async-done | bytes 2097184 | tf_op jit(solution)/shard_map/all_to_all | solution.py:24
  136.3 1.0 copy-done.9
  137.3 0.9 copy-done.11
  138.3 0.7 copy-done.12
  139.0 9.6 %shard_map.183 = bf16[128,512]{1,0:T(8,128)(2,1)} custom-call(bf16[2048,512]{1,0:T(8,128)(2,1)} %bitcast.13.refs_0_, bf16[2048,128]{1,0:T(8,128)(2,1)} %cosine_convert_fusion.1.refs_1_, s32[1,2048]{1,0:T(1,128)S(1)} %copy-done.12, bf16[128,512]{1,0:T(8,128)(2,1)S(1)} %get-tuple-element.26.refs_3_, bf16[640,1024]{1,0:T(8,128)(2,1)S(1)} %copy-done.4, ...), custom_call_target="tpu_custom_call" | custom-call | tf_op jit(solution)/shard_map/pallas_call | solution.py:330
  148.7 8.2 %shard_map.184 = bf16[2048,512]{1,0:T(8,128)(2,1)} custom-call(bf16[128,16,512]{2,1,0:T(8,128)(2,1)} %all-to-all-done.2.msgs_ref, bf16[512,512]{1,0:T(8,128)(2,1)} %shard_map.179.old_ref, f32[512,1536]{1,0:T(8,128)} %convolution_add_fusion.gh_ref, s32[1,512]{1,0:T(1,128)S(1)} %copy-done.16, s32[1,1024]{1,0:T(1,128)S(1)} %copy-done.15, ...), custom_call_target="tpu_custom_call" | custom-call | tf_op jit(solution)/shard_map/pallas_call | solution.py:255
  (54 shorter events, 1.1 us)
Async XLA Ops:
  0.6 70.3 %copy-start = (bf16[512,1536]{1,0:T(8,128)(2,1)S(1)}, bf16[512,1536]{1,0:T(8,128)(2,1)}, u32[]{:S(2)}) copy-start(bf16[512,1536]{1,0:T(8,128)(2,1)} %param.32) | copy-start | bytes 4718596
  3.5 20.9 %all-to-all-start = ((s32[128,1,128]{2,1,0:T(1,128)}), s32[128,1,128]{2,1,0:T(1,128)S(1)}, u32[]{:S(2)}, u32[]{:S(2)}) async-start(s32[128,1,128]{2,1,0:T(1,128)} %bitcast.5), calls=%async_computation | async-start | bytes 131072 | tf_op jit(solution)/shard_map/all_to_all | solution.py:24
  17.0 2.0 %copy-start.1 = (f32[8192,128]{1,0:T(8,128)}, f32[8192,128]{1,0:T(8,128)S(1)}, u32[]{:S(2)}) copy-start(f32[8192,128]{1,0:T(8,128)S(1)} %shard_map.177.mem_ref) | copy-start | bytes 12582916
  24.4 0.6 copy-start.19
  25.1 2.2 %copy-start.2 = (f32[8192,128]{1,0:T(8,128)S(1)}, f32[8192,128]{1,0:T(8,128)}, u32[]{:S(2)}) copy-start(f32[8192,128]{1,0:T(8,128)} %copy-done.1) | copy-start | bytes 12582916
  36.1 5.6 %copy-start.23 = (s32[128]{0:T(128)S(1)}, s32[128]{0:T(128)}, u32[]{:S(2)}) copy-start(s32[128]{0:T(128)} %param.19) | copy-start | bytes 1540
  36.1 7.3 %copy-start.13 = (f32[2,1536]{1,0:T(2,128)S(1)}, f32[2,1536]{1,0:T(2,128)}, u32[]{:S(2)}) copy-start(f32[2,1536]{1,0:T(2,128)} %bias_ref.1) | copy-start | bytes 36868
  36.1 7.4 %copy-start.21 = (f32[128]{0:T(128)S(1)}, f32[128]{0:T(128)}, u32[]{:S(2)}) copy-start(f32[128]{0:T(128)} %param.23) | copy-start | bytes 1540
  36.1 7.4 %copy-start.22 = (f32[128]{0:T(128)S(1)}, f32[128]{0:T(128)}, u32[]{:S(2)}) copy-start(f32[128]{0:T(128)} %param.22) | copy-start | bytes 1540
  36.1 58.2 %all-to-all-start.1 = ((bf16[128,32,512]{2,1,0:T(8,128)(2,1)}), bf16[128,32,512]{2,1,0:T(8,128)(2,1)}, u32[]{:S(2)}, u32[]{:S(2)}) async-start(bf16[128,32,512]{2,1,0:T(8,128)(2,1)} %bitcast.24), calls=%async_computation.1 | async-start | bytes 8388608 | tf_op jit(solution)/shard_map/all_to_all | solution.py:24
  41.7 15.4 %copy-start.20 = (s32[128,1,128]{2,1,0:T(1,128)S(1)}, s32[128,1,128]{2,1,0:T(1,128)}, u32[]{:S(2)}) copy-start(s32[128,1,128]{2,1,0:T(1,128)} %copy-done.19) | copy-start | bytes 196612
  57.9 2.2 %copy-start.3 = (f32[8192,128]{1,0:T(8,128)S(1)}, f32[8192,128]{1,0:T(8,128)}, u32[]{:S(2)}) copy-start(f32[8192,128]{1,0:T(8,128)} %copy-done.1) | copy-start | bytes 12582916
  70.9 23.4 %copy-start.7 = (bf16[1024,512]{1,0:T(8,128)(2,1)S(1)}, bf16[1024,512]{1,0:T(8,128)(2,1)}, u32[]{:S(2)}) copy-start(bf16[1024,512]{1,0:T(8,128)(2,1)} %w2_ref.1) | copy-start | bytes 3145732
  70.9 23.4 %copy-start.8 = (bf16[512,512]{1,0:T(8,128)(2,1)S(1)}, bf16[512,512]{1,0:T(8,128)(2,1)}, u32[]{:S(2)}) copy-start(bf16[512,512]{1,0:T(8,128)(2,1)} %wq_ref.1) | copy-start | bytes 1572868
  70.9 23.4 %copy-start.17 = (f32[1024]{0:T(1024)S(1)}, f32[1024]{0:T(1024)}, u32[]{:S(2)}) copy-start(f32[1024]{0:T(1024)} %param.25) | copy-start | bytes 12292
  70.9 23.4 %copy-start.18 = (f32[512]{0:T(512)S(1)}, f32[512]{0:T(512)}, u32[]{:S(2)}) copy-start(f32[512]{0:T(512)} %param.27) | copy-start | bytes 6148
  94.4 1.7 %copy-start.5 = (bf16[1152,1024]{1,0:T(8,128)(2,1)S(1)}, bf16[1152,1024]{1,0:T(8,128)(2,1)}, u32[]{:S(2)}) copy-start(bf16[1152,1024]{1,0:T(8,128)(2,1)} %w1_ref.1) | copy-start | bytes 7077892
  100.4 6.0 %copy-start.4 = (bf16[640,1024]{1,0:T(8,128)(2,1)S(1)}, bf16[640,1024]{1,0:T(8,128)(2,1)}, u32[]{:S(2)}) copy-start(bf16[640,1024]{1,0:T(8,128)(2,1)} %refs_4_.3) | copy-start | bytes 3932164
  100.4 35.9 %all-to-all-start.2 = ((bf16[128,16,512]{2,1,0:T(8,128)(2,1)}), bf16[128,16,512]{2,1,0:T(8,128)(2,1)}, u32[]{:S(2)}, u32[]{:S(2)}) async-start(bf16[128,16,512]{2,1,0:T(8,128)(2,1)} %get-tuple-element.23), calls=%async_computation.2 | async-start | bytes 4194304 | tf_op jit(solution)/shard_map/all_to_all | solution.py:24
  122.4 0.7 copy-start.10
  136.3 1.0 copy-start.9
  137.3 0.9 copy-start.11
  138.3 0.7 copy-start.12
  139.0 9.6 %copy-start.6 = (bf16[512,1536]{1,0:T(8,128)(2,1)S(1)}, bf16[512,1536]{1,0:T(8,128)(2,1)}, u32[]{:S(2)}) copy-start(bf16[512,1536]{1,0:T(8,128)(2,1)} %wi_ref.1) | copy-start | bytes 4718596
  139.0 9.6 %copy-start.14 = (f32[2,1536]{1,0:T(2,128)S(1)}, f32[2,1536]{1,0:T(2,128)}, u32[]{:S(2)}) copy-start(f32[2,1536]{1,0:T(2,128)} %bias_ref.1) | copy-start | bytes 36868
  139.0 9.6 %copy-start.15 = (s32[1,1024]{1,0:T(1,128)S(1)}, s32[1,1024]{1,0:T(1,128)}, u32[]{:S(2)}) copy-start(s32[1,1024]{1,0:T(1,128)} %reshape.58.to_t_ref) | copy-start | bytes 12292
  139.0 9.6 %copy-start.16 = (s32[1,512]{1,0:T(1,128)S(1)}, s32[1,512]{1,0:T(1,128)}, u32[]{:S(2)}) copy-start(s32[1,512]{1,0:T(1,128)} %reshape.57.to_c_ref) | copy-start | bytes 6148

commit v2 on v1

v2 whole, which is shorter than its diff:
```python
import functools

import jax
import jax.numpy as jnp
from jax import lax
from jax.experimental import pallas as pl
from jax.experimental.pallas import tpu as pltpu
from jax.sharding import PartitionSpec as P

HDIM = 128
LANES = 128
AXES = ("grp", "dev")
F32 = jnp.float32
BF16 = jnp.bfloat16
NEG = -1e30
NT = (((1,), (1,)), ((), ()))


def dotf(a, b):
    return jnp.dot(a, b, preferred_element_type=F32)


def exchange(x):
    return lax.all_to_all(x, AXES, split_axis=0, concat_axis=0, tiled=True)


def call(kernel, out_shape, *args, scalars=0, scratch=(), mib=16):
    return pl.pallas_call(
        kernel,
        out_shape=out_shape,
        grid_spec=pltpu.PrefetchScalarGridSpec(
            num_scalar_prefetch=scalars,
            grid=(),
            in_specs=[pl.BlockSpec(memory_space=pltpu.VMEM)] * (len(args) - scalars),
            out_specs=jax.tree.map(lambda _: pl.BlockSpec(memory_space=pltpu.VMEM), out_shape),
            scratch_shapes=scratch,
        ),
        compiler_params=pltpu.CompilerParams(vmem_limit_bytes=mib << 20),
    )(*args)


def hbm(x):
    return pltpu.with_memory_space_constraint(x, pltpu.HBM)


def vmem(x):
    return pltpu.with_memory_space_constraint(x, pltpu.VMEM)


def whole(x):
    zeros = (0,) * x.ndim
    return pl.BlockSpec(x.shape, lambda *_: zeros)


def sds(shape, dtype):
    return jax.ShapeDtypeStruct(shape, dtype)


def place_kernel(shift, parts, cap_n, rows, nid_ref, nt_ref, en_ref, tick_ref, req_ref, map_ref, dt_ref):
    fanout, events = nid_ref.shape
    owners = req_ref.shape[0]
    i0 = lax.broadcasted_iota(jnp.int32, (owners, events), 0)
    e0 = lax.broadcasted_iota(jnp.int32, (events, events), 0)
    e1 = lax.broadcasted_iota(jnp.int32, (events, events), 1)
    tri = jnp.where(e0 <= e1, 1.0, 0.0)
    both = jnp.concatenate([tri, jnp.ones((events, events), F32)], axis=1).astype(BF16)
    srow = lax.broadcasted_iota(jnp.int32, (rows, events), 0)
    lane = lax.broadcasted_iota(jnp.int32, (1, events), 1)
    tick = tick_ref[...]
    mask = (1 << shift) - 1
    acc = jnp.zeros((6 * rows, owners), F32)
    base = jnp.zeros((owners, events), F32)
    zero = jnp.zeros((1, events), jnp.int32)
    for k in range(fanout + 2):
        near = k < fanout
        if k == fanout:
            base = jnp.zeros((owners, events), F32)
        ids = nid_ref[k : k + 1, :] if near else en_ref[k - fanout : k - fanout + 1, :]
        local = jnp.bitwise_and(ids, mask)
        hit = i0 == jnp.right_shift(ids, shift)
        onehot = jnp.where(hit, 1.0, 0.0)
        ohb = onehot.astype(BF16)
        ranks = dotf(ohb, both)
        cum = ranks[:, :events] + base
        base = base + ranks[:, events:]
        slot = jnp.sum(onehot * cum, axis=0, keepdims=True).astype(jnp.int32) - 1
        if near:
            d = tick - nt_ref[k : k + 1, :] + 131072
            code = lane + 1
            digits = (d & 255, jnp.right_shift(d, 8) & 255, jnp.right_shift(d, 16))
            value = local * parts
        else:
            slot = slot + cap_n
            code = lane + (1 + events * (k - fanout))
            digits = (zero, zero, zero)
            value = (local + 1) * parts
        vals = (value & 255, jnp.right_shift(value, 8), code) + digits
        so = srow == slot
        table = jnp.concatenate([jnp.where(so, v.astype(F32), 0.0) for v in vals], axis=0)
        acc = acc + lax.dot_general(table.astype(BF16), ohb, NT, preferred_element_type=F32)
    a = [acc[i * rows : (i + 1) * rows] for i in range(6)]
    pad = jnp.zeros((LANES - rows, owners), F32)

    def turned(x):
        return jnp.concatenate([x, pad], axis=0).T

    req_ref[...] = turned(a[0] + 256.0 * a[1]).astype(jnp.int32)
    map_ref[...] = turned(a[2]).astype(jnp.int32)
    dt = a[3] + 256.0 * a[4] + 65536.0 * a[5] - 131072.0
    dt_ref[...] = turned(jnp.where(a[2] > 0.0, dt, 0.0))


def spread(src_ref, dst_ref, base=0):
    rows, width = src_ref.shape
    parts = width // LANES
    block = 128

    def step(i, carry):
        r = pl.multiple_of(i * block, block)
        for c in range(parts):
            part = src_ref[pl.ds(r, block), c * LANES : (c + 1) * LANES].astype(F32)
            dst_ref[pl.ds(base + r * parts + c, block, stride=parts), :] = part
        return carry

    lax.fori_loop(0, rows // block, step, 0)


def gather_back(src_ref, base, dst_ref, row, rows):
    parts = dst_ref.shape[1] // LANES
    for c in range(parts):
        part = src_ref[pl.ds(base + c, rows, stride=parts), :]
        dst_ref[pl.ds(row, rows), c * LANES : (c + 1) * LANES] = part.astype(dst_ref.dtype)


def pick_group(n):
    return 16 // n if n < 16 else 2


def pick_kernel(cols, shifted, req_ref, mem_ref, out_ref, req_s, mem_v, mem32, stage, out_v, sems):
    peers = req_ref.shape[0]
    width = mem_ref.shape[1]
    parts = width // LANES
    n = len(cols)
    blocks = out_v.shape[0]
    group = pick_group(n)
    total = n * group
    steps = peers // group // blocks
    load_mem = pltpu.make_async_copy(mem_ref, mem_v, sems.at[0])
    load_req = pltpu.make_async_copy(req_ref, req_s, sems.at[1])
    load_mem.start()
    load_req.start()
    load_mem.wait()
    spread(mem_v, mem32)
    load_req.wait()
    copies = []
    for b in range(blocks):

        def step(i, carry):
            for g in range(group):
                o = (b * steps + i) * group + g
                for j, col in enumerate(cols):
                    at = req_s[o, col]
                    if shifted[j]:
                        at = jnp.maximum(at - parts, 0)
                    at = pl.multiple_of(at, parts)
                    s = (g * n + j) * parts
                    stage[s : s + parts, :] = mem32[pl.ds(at, parts), :]
            r = pl.multiple_of(i * total, total)
            gather_back(stage, 0, out_v.at[b], r, total)
            return carry

        lax.fori_loop(0, steps, step, 0)
        size = steps * total
        copy = pltpu.make_async_copy(out_v.at[b], out_ref.at[pl.ds(b * size, size)], sems.at[2 + b])
        copy.start()
        copies.append(copy)
    for copy in copies:
        copy.wait()


def pick(req, memory, cols, shifted, blocks=4):
    peers = req.shape[0]
    nodes, width = memory.shape
    parts = width // LANES
    rows = peers * len(cols)
    anywhere = pl.BlockSpec(memory_space=pl.ANY)
    return pl.pallas_call(
        functools.partial(pick_kernel, cols, shifted),
        out_shape=pltpu.HBM((rows, width), BF16),
        in_specs=[anywhere, anywhere],
        out_specs=anywhere,
        scratch_shapes=[
            pltpu.SMEM(req.shape, jnp.int32),
            pltpu.VMEM((nodes, width), BF16),
            pltpu.VMEM((nodes * parts, LANES), F32),
            pltpu.VMEM((len(cols) * pick_group(len(cols)) * parts, LANES), F32),
            pltpu.VMEM((blocks, rows // blocks, width), BF16),
            pltpu.SemaphoreType.DMA((2 + blocks,)),
        ],
        compiler_params=pltpu.CompilerParams(vmem_limit_bytes=16 << 20),
    )(hbm(req), hbm(memory))


def starts(pairs, sems):
    copies = [pltpu.make_async_copy(src, dst, sems.at[i]) for i, (src, dst) in enumerate(pairs)]
    for copy in copies:
        copy.start()
    return copies


def message_kernel(cap_e, *refs):
    ins = refs[:9]
    out_ref, q_ref = refs[9:11]
    rows, code, w1, enc, b1, w2, b2, base, wq, out_v, q_v, sems = refs[11:]
    peers, per, width = rows.shape
    slots = peers * per
    events = enc.shape[0]
    sources = (ins[0].at[:, 0:per, :],) + tuple(ins[1:])
    loads = starts(list(zip(sources, (rows, code, w1, enc, b1, w2, b2, base, wq))), sems)
    loads[1].wait()
    target = lax.broadcasted_iota(jnp.int32, (2 * events, slots), 0) + 1
    sel = jnp.where(target == code[...], 1.0, 0.0)
    loads[0].wait()
    pair = dotf(sel.astype(BF16), rows[...].reshape(slots, width)).astype(BF16)
    for i in (2, 3, 4):
        loads[i].wait()
    first = dotf(pair, w1[:width, :])
    second = dotf(pair, w1[width : 2 * width, :])
    third = dotf(enc[...], w1[2 * width :, :]) + b1[...]
    both = jnp.concatenate([second[events:] + third, second[:events] + third], axis=0)
    hidden = jnp.maximum(first + both, 0.0).astype(BF16)
    for i in (5, 6):
        loads[i].wait()
    msg = (dotf(hidden, w2[...]) + b2[...]).astype(BF16)
    placed = dotf(sel.T.astype(BF16), msg)
    j = lax.broadcasted_iota(jnp.int32, (slots, width), 0) & (per - 1)
    loads[7].wait()
    kept = base[...].reshape(slots, width).astype(F32)
    out_v[...] = jnp.where(j < cap_e, placed, kept).astype(BF16).reshape(peers, per, width)
    store = pltpu.make_async_copy(out_v, out_ref, sems.at[9])
    store.start()
    loads[8].wait()
    q_v[...] = dotf(pair[:events], wq[...]).astype(BF16)
    store_q = pltpu.make_async_copy(q_v, q_ref, sems.at[10])
    store_q.start()
    store.wait()
    store_q.wait()


def messages(cap_e, got, code, w1, enc, b1, w2, b2, base, wq):
    peers, _, width = got.shape
    args = (got, code, w1, enc, b1, w2, b2, base, wq)
    q_shape = (enc.shape[0], width)
    tile = (peers, 8, width)
    anywhere = pl.BlockSpec(memory_space=pl.ANY)
    scratch = [pltpu.VMEM(tile, BF16)] + [pltpu.VMEM(x.shape, x.dtype) for x in args[1:]]
    scratch += [pltpu.VMEM(tile, BF16), pltpu.VMEM(q_shape, BF16), pltpu.SemaphoreType.DMA((11,))]
    return pl.pallas_call(
        functools.partial(message_kernel, cap_e),
        out_shape=(pltpu.HBM(base.shape, BF16), pltpu.HBM(q_shape, BF16)),
        in_specs=[anywhere] * len(args),
        out_specs=(anywhere, anywhere),
        scratch_shapes=scratch,
        compiler_params=pltpu.CompilerParams(vmem_limit_bytes=28 << 20),
    )(*[hbm(x) for x in args])


def prepare_kernel(to_c_ref, to_t_ref, old_ref, wh_ref, bias_ref, hits_ref, inv_ref, gh_ref):
    slots = old_ref.shape[0]
    row = to_c_ref[...].astype(F32)
    col = jnp.broadcast_to(row, (8, slots)).T[:, 0:1]
    tiles = to_t_ref[...].astype(F32)
    hits = jnp.where(jnp.logical_and(col == tiles, tiles > 0.0), 1.0, 0.0)
    counts = jnp.sum(hits, axis=1, keepdims=True)
    hits_ref[...] = hits.astype(BF16)
    inv_ref[...] = jnp.broadcast_to(jnp.maximum(counts, 1.0), inv_ref.shape)
    gh_ref[...] = (dotf(old_ref[...], wh_ref[...]) + bias_ref[1:2, :]).astype(BF16)


def prepare(to_c, to_t, old, wh, bias):
    slots = old.shape[0]
    args = (to_c, to_t, hbm(old), wh, bias)
    out = ((slots, to_t.shape[1]), BF16), ((slots, LANES), F32), ((slots, wh.shape[1]), BF16)
    return pl.pallas_call(
        prepare_kernel,
        out_shape=tuple(pltpu.HBM(*x) for x in out),
        grid=(1,),
        in_specs=[whole(x) for x in args],
        out_specs=tuple(whole(sds(*x)) for x in out),
        compiler_params=pltpu.CompilerParams(vmem_limit_bytes=24 << 20),
    )(*args)


def block_scores(qk_ref, rows, enc, slot_map, events):
    slots, width = rows.shape
    heads = qk_ref.shape[0] // events
    s = lax.dot_general(qk_ref[:, :width], rows, NT, preferred_element_type=F32)
    s = s + lax.dot_general(qk_ref[:, width:], enc, NT, preferred_element_type=F32)
    event = lax.broadcasted_iota(jnp.int32, (events, slots), 0) + 1
    bias = jnp.where(event == slot_map, 0.0, NEG)
    return s + jnp.concatenate([bias] * heads, axis=0)


def block_sums(p, rows, enc):
    slots = rows.shape[0]
    tail = jnp.concatenate([enc, jnp.ones((slots, LANES), BF16)], axis=1)
    return dotf(p, rows), dotf(p, tail)


def attend_kernel(rows_ref, enc_ref, map_ref, q_ref, w_ref, qk_ref, m_ref, a_ref):
    slots, width = rows_ref.shape
    events = q_ref.shape[0]

    @pl.when(pl.program_id(0) == 0)
    def _():
        scale = 1.4426950408889634 / HDIM**0.5
        for h in range(width // HDIM):
            cut = slice(h * HDIM, (h + 1) * HDIM)
            qk = lax.dot_general(q_ref[:, cut], w_ref[:, cut], NT, preferred_element_type=F32)
            qk_ref[h * events : (h + 1) * events, :] = (qk * scale).astype(BF16)
        m_ref[...] = jnp.full(m_ref.shape, NEG, F32)
        a_ref[...] = jnp.zeros(a_ref.shape, F32)

    rows = rows_ref[...]
    enc = enc_ref[...]
    s = block_scores(qk_ref, rows, enc, map_ref[...], events)
    m_old = m_ref[...]
    m = jnp.maximum(m_old, jnp.max(s, axis=1, keepdims=True))
    p = jnp.exp2(s - m[:, 0:1]).astype(BF16)
    scale = jnp.exp2(m_old - m)[:, 0:1]
    m_ref[...] = m
    near, far = block_sums(p, rows, enc)
    a_ref[:, :width] = scale * a_ref[:, :width] + near
    a_ref[:, width:] = scale * a_ref[:, width:] + far


def attend(rows, enc, slot_map, query, w):
    total, width = rows.shape
    block = 1024
    events = query.shape[0]
    stacked = width // HDIM * events
    shapes = (
        ((stacked, width + LANES), BF16),
        ((stacked, LANES), F32),
        ((stacked, width + 2 * LANES), F32),
    )
    return pl.pallas_call(
        attend_kernel,
        out_shape=tuple(pltpu.HBM(*x) for x in shapes),
        grid=(total // block,),
        in_specs=[
            pl.BlockSpec((block, width), lambda i: (i, 0)),
            pl.BlockSpec((block, LANES), lambda i: (i, 0)),
            pl.BlockSpec((1, block), lambda i: (0, i)),
            whole(query),
            pl.BlockSpec((w.shape[0], width), lambda i: (0, 0)),
        ],
        out_specs=tuple(whole(sds(*x)) for x in shapes),
        compiler_params=pltpu.CompilerParams(vmem_limit_bytes=28 << 20),
    )(hbm(rows), hbm(enc), hbm(slot_map), hbm(query), hbm(w))


def finish_kernel(*refs):
    ins = refs[:16]
    emb_ref, out_ref = refs[16:18]
    (got, enc, slot_map, qk, m_prev, a_prev, w, wo, hits, inv, wi, bias, gh, old, mem, to) = refs[18:34]
    tile32, near, msgs, emb_v, mem32, fresh32, out_v, sems = refs[34:]
    peers, per, width = got.shape
    slots = old.shape[0]
    cap = slots // peers
    nodes = mem.shape[0]
    parts = width // LANES
    blocks = out_v.shape[0]
    inner = w.shape[0]
    heads = width // HDIM
    events = qk.shape[0] // heads
    sources = list(ins)
    sources[6] = ins[6].at[:, pl.ds(width, width)]
    loads = starts(list(zip(sources, refs[18:34])), sems)
    loads[0].wait()
    flat = got[...].reshape(peers * per, width)
    for c in range(parts):
        tile32[c] = flat[:, c * LANES : (c + 1) * LANES].astype(F32)
    for dst, off in ((near, cap), (msgs, 0)):
        for j in range(cap):
            for c in range(parts):
                part = tile32[c, pl.ds(off + j, peers, stride=per), :]
                dst[j * peers : (j + 1) * peers, c * LANES : (c + 1) * LANES] = part.astype(BF16)
    for i in range(1, 4):
        loads[i].wait()
    s = block_scores(qk, near[...], enc[...], slot_map[...], events)
    m_new = jnp.max(s, axis=1, keepdims=True)
    p = jnp.exp2(s - m_new).astype(BF16)
    rows_sum, tail_sum = block_sums(p, near[...], enc[...])
    loads[4].wait()
    loads[5].wait()
    before = m_prev[:, 0:1]
    m = jnp.maximum(m_new, before)
    f_new = jnp.exp2(m_new - m)
    f_old = jnp.exp2(before - m)
    part_a = f_new * rows_sum + f_old * a_prev[:, :width]
    part_b = f_new * tail_sum + f_old * a_prev[:, width:]
    total = part_b[:, LANES : LANES + 1]
    mixed_a = (part_a / total).astype(BF16)
    mixed_b = (part_b[:, :LANES] / total).astype(BF16)
    loads[6].wait()
    loads[7].wait()
    outs = []
    for h in range(heads):
        cut = slice(h * HDIM, (h + 1) * HDIM)
        at = slice(h * events, (h + 1) * events)
        value = dotf(mixed_a[at], w[:width, cut]) + dotf(mixed_b[at], w[width:, cut])
        outs.append(value.astype(BF16))
    emb_v[...] = dotf(jnp.concatenate(outs, axis=1), wo[...]).astype(BF16)
    copies = [pltpu.make_async_copy(emb_v, emb_ref, sems.at[16])]
    copies[0].start()

    for i in range(8, 12):
        loads[i].wait()
    sums = dotf(hits[...], msgs[...])
    mean = (sums / inv[:, 0:1]).astype(BF16)
    gi = dotf(mean, wi[...]) + bias[0:1, :]
    loads[12].wait()
    loads[13].wait()
    r = jax.nn.sigmoid(gi[:, :width] + gh[:, :width].astype(F32))
    z = jax.nn.sigmoid(gi[:, width : 2 * width] + gh[:, width : 2 * width].astype(F32))
    c = jnp.tanh(gi[:, 2 * width :] + r * gh[:, 2 * width :].astype(F32))
    fresh = (1.0 - z) * c + z * old[...].astype(F32)
    for k in range(parts):
        fresh32[pl.ds(k, slots, stride=parts), :] = fresh[:, k * LANES : (k + 1) * LANES]
    loads[14].wait()
    spread(mem, mem32, parts)
    loads[15].wait()

    def step(i, carry):
        for k in range(16):
            s = i * 16 + k
            at = pl.multiple_of(to[s], parts)
            mem32[pl.ds(at, parts), :] = fresh32[pl.ds(pl.multiple_of(s * parts, parts), parts), :]
        return carry

    lax.fori_loop(0, slots // 16, step, 0)
    size = nodes // blocks
    for b in range(blocks):

        def back(i, carry):
            row = pl.multiple_of(i * 128, 128)
            gather_back(mem32, parts + (b * size + row) * parts, out_v.at[b], row, 128)
            return carry

        lax.fori_loop(0, size // 128, back, 0)
        copy = pltpu.make_async_copy(out_v.at[b], out_ref.at[pl.ds(b * size, size)], sems.at[17 + b])
        copy.start()
        copies.append(copy)
    for copy in copies:
        copy.wait()


def finish(got, enc, slot_map, qk, m, a, w, wo, hits, inv, wi, bias, gh, old, memory, to, blocks=4):
    args = (got, enc, slot_map, qk, m, a, w, wo, hits, inv, wi, bias, gh, old, memory, to)
    peers, per, width = got.shape
    nodes = memory.shape[0]
    slots = old.shape[0]
    parts = width // LANES
    emb_shape = (qk.shape[0] // (width // HDIM), width)
    anywhere = pl.BlockSpec(memory_space=pl.ANY)
    shapes = [x.shape for x in args[:-1]]
    shapes[6] = (w.shape[0], width)
    scratch = [pltpu.VMEM(shape, x.dtype) for shape, x in zip(shapes, args)]
    scratch += [
        pltpu.SMEM(to.shape, jnp.int32),
        pltpu.VMEM((parts, peers * per, LANES), F32),
        pltpu.VMEM((slots, width), BF16),
        pltpu.VMEM((slots, width), BF16),
        pltpu.VMEM(emb_shape, BF16),
        pltpu.VMEM(((nodes + 1) * parts, LANES), F32),
        pltpu.VMEM((slots * parts, LANES), F32),
        pltpu.VMEM((blocks, nodes // blocks, width), BF16),
        pltpu.SemaphoreType.DMA((17 + blocks,)),
    ]
    return pl.pallas_call(
        finish_kernel,
        out_shape=(pltpu.HBM(emb_shape, BF16), pltpu.HBM(memory.shape, BF16)),
        in_specs=[anywhere] * len(args),
        out_specs=(anywhere, anywhere),
        scratch_shapes=scratch,
        compiler_params=pltpu.CompilerParams(vmem_limit_bytes=44 << 20),
    )(*[hbm(x) for x in args])


def encode(dt, freq, phase):
    return jnp.cos(dt[..., None] * freq + phase).astype(BF16)


def on_device(
    memory,
    event_nodes,
    event_ticks,
    neighbour_ids,
    neighbour_ticks,
    freq,
    phase,
    w_msg1,
    b_msg1,
    w_msg2,
    b_msg2,
    w_query,
    w_keyval,
    w_out,
    gru_input,
    gru_hidden,
    gru_bias,
):
    owners = lax.axis_size(AXES)
    nodes, width = memory.shape
    events, fanout = neighbour_ids.shape
    cap_e = 4 * events // owners
    cap_n = 2 * fanout * events // owners
    rows = cap_n + 8
    shift = nodes.bit_length() - 1
    assert nodes == 1 << shift and cap_e == 4 and cap_n == 40
    table = (owners, LANES)
    req, owner_map, dt = call(
        functools.partial(place_kernel, shift, width // LANES, cap_n, rows),
        (sds(table, jnp.int32), sds(table, jnp.int32), sds(table, F32)),
        hbm(neighbour_ids.T),
        hbm(neighbour_ticks.T),
        hbm(event_nodes.T),
        hbm(event_ticks.reshape(1, events)),
        mib=8,
    )
    asked = exchange(req)

    half = 8 - cap_e
    near = cap_n - half
    ev = tuple(range(cap_n, cap_n + cap_e))
    cols_a = ev + tuple(range(near))
    cols_c = tuple(range(near, near + cap_e)) + tuple(range(near, cap_n))
    take = functools.partial(pick, asked, memory)
    sent_a = take(cols_a, (True,) * cap_e + (False,) * near)
    got_a = exchange(sent_a)
    base_c = take(cols_c, (False,) * len(cols_c)).reshape(owners, -1, width)
    old = take(ev, (True,) * cap_e)

    def spaced(x):
        return jnp.concatenate([jnp.zeros((owners, cap_e), x.dtype), x], axis=1)

    def tiled(x):
        return jnp.concatenate([x, jnp.zeros((owners, half), x.dtype)], axis=1).reshape(1, -1)

    code = tiled(owner_map[:, cap_n : cap_n + cap_e])
    map_a = spaced(owner_map[:, :near]).reshape(1, -1)
    map_c = owner_map[:, near:cap_n].T.reshape(1, -1)
    to = asked[:, cap_n : cap_n + cap_e]
    to_s = to.reshape(-1)
    hits, counts, gh = prepare(to.reshape(1, -1), to.T.reshape(1, -1), old, gru_hidden, gru_bias)
    enc_a = encode(spaced(dt[:, :near]), freq, phase).reshape(-1, LANES)
    enc_c = encode(dt[:, near:cap_n].T, freq, phase).reshape(-1, LANES)
    enc = encode(event_ticks.astype(F32), freq, phase)
    got_a, enc_a, enc_c, map_a, map_c, hits, counts, gh, base_c, to_s = lax.optimization_barrier(
        (got_a, enc_a, enc_c, map_a, map_c, hits, counts, gh, base_c, to_s)
    )
    sent_c, query = messages(
        cap_e,
        got_a.reshape(owners, -1, width),
        code,
        w_msg1,
        enc,
        b_msg1.reshape(1, -1),
        w_msg2,
        b_msg2.reshape(1, -1),
        base_c,
        w_query,
    )
    got_c = exchange(sent_c)
    qk, m, a = attend(got_a, enc_a, map_a, query, w_keyval)
    return finish(
        got_c,
        enc_c,
        map_c,
        qk,
        m,
        a,
        w_keyval,
        w_out,
        hits,
        counts,
        gru_input,
        gru_bias,
        gh,
        old,
        memory,
        to_s,
    )


def solution(mesh):
    split = P(AXES, None)
    in_specs = (split, split, P(AXES), split, split) + (P(),) * 12
    return jax.shard_map(
        on_device, mesh=mesh, in_specs=in_specs, out_specs=(split, split), check_vma=False
    )
```

time: 158 us -> 144 us (0.911)
  blocking collectives: 0 us -> 21.1 us
  starting transfers between devices: 23.1 us -> 12 us
  local copies, waits for them, and re-layouts: 15.3 us -> 4.56 us
  Pallas kernels: 62 us -> 54.4 us
  matrix products: 3.79 us -> 0 us
    all_to_all x0 -> x1, blocking collectives: none -> 21.1 us  [exchange(): return lax.all_to_all(x, AXES, split_axis=0, concat_axis=0, tiled=True)]
    unnamed x48 -> x14, local copies, waits for them, and re-layouts: 12.1 us -> 1.01 us
    all_to_all x3 -> x2, starting transfers between devices: 23.1 us -> 12 us  [exchange(): return lax.all_to_all(x, AXES, split_axis=0, concat_axis=0, tiled=True)]
    pallas_call x3, Pallas kernels: 33.8 us -> 30 us  [the longest x1 18.2 us: attend(): pl.pallas_call(attend_kernel, out_shape=tuple((pltpu.HBM(*x) for x in sha...]
    dot_general x1 -> x0, matrix products: 3.79 us -> none  [on_device(): gh = jnp.dot(old, gru_hidden, preferred_element_type=F32) + gru_bias[1]]
    pallas_call x2 -> x1, Pallas kernels: 4.86 us -> 2.14 us  [call(): pl.pallas_call(kernel, out_shape=out_shape, grid_spec=pltpu.PrefetchScala...]
    pallas_call x3, Pallas kernels: 18.9 us -> 17.3 us  [pick(): pl.pallas_call(functools.partial(pick_kernel, cols, shifted), out_shape=p...]
    all_to_all x3 -> x2, waiting for transfers between devices: 38.2 us -> 37 us  [exchange(): return lax.all_to_all(x, AXES, split_axis=0, concat_axis=0, tiled=True)]
  transfers between devices with their start and end apart: 3 -> 2, of which waited for: 3 -> 2; matrix products, arithmetic and copies ran while one was open for 13% -> 12% of each run, Pallas kernels for 18% -> 21%
where the time goes in v2:
time: 144 us; the launch traced here: 143 us
  Pallas kernels  54.4 us (38%)
  waiting for transfers between devices  37 us (26%)
  blocking collectives  21.1 us (15%)
  other arithmetic  13.2 us (9%)
  starting transfers between devices  12 us (8%)
  local copies, waits for them, and re-layouts  4.56 us (3%)
    all_to_all x2, waiting for transfers between devices, exchange(): return lax.all_to_all(x, AXES, split_axis=0, concat_axis=0, tiled=True)  37 us
    all_to_all x1, blocking collectives, exchange(): return lax.all_to_all(x, AXES, split_axis=0, concat_axis=0, tiled=True)  21.1 us
    pallas_call x1, Pallas kernels, attend(): pl.pallas_call(attend_kernel, out_shape=tuple((pltpu.HBM(*x) for x in sha...  18.2 us
    pallas_call x3, Pallas kernels, pick(): pl.pallas_call(functools.partial(pick_kernel, cols, shifted), out_shape=p...  17.3 us
    convert_element_type x3, other arithmetic, encode(): return jnp.cos(dt[..., None] * freq + phase).astype(BF16)  13.2 us
    all_to_all x2, starting transfers between devices, exchange(): return lax.all_to_all(x, AXES, split_axis=0, concat_axis=0, tiled=True)  12 us
    pallas_call x1, Pallas kernels, finish(): pl.pallas_call(finish_kernel, out_shape=(pltpu.HBM(emb_shape, BF16), pltp...  8.54 us
    pallas_call x1, Pallas kernels, messages(): pl.pallas_call(functools.partial(message_kernel, cap_e), out_shape=(pltpu...  4.93 us
  transfers between devices with their start and end apart: 2, of which 2 were waited for; matrix products, arithmetic and copies ran while one was open for 12% of the time, Pallas kernels for 21%

profile of v2, /device:TPU:1, one launch (start us, length us, event | category | flops | bytes accessed | tf_op | source)
XLA Modules:
  0.0 143.2 jit_solution(15596995396906501389)
XLA Ops:
  0.6 2.1 %shard_map.176 = (s32[128,128]{1,0:T(8,128)S(1)}, s32[128,128]{1,0:T(8,128)S(1)}, f32[128,128]{1,0:T(8,128)S(1)}) custom-call(s32[20,128]{1,0:T(8,128)} %bitcast.35, s32[20,128]{1,0:T(8,128)} %bitcast.36, s32[2,128]{1,0:T(2,128)} %bitcast.41, s32[1,128]{1,0:T(1,128)} %bitcast.42), custom_call_target="tpu_custom_call" | custom-call | tf_op jit(solution)/shard_map/pallas_call | solution.py:28
  2.8 21.1 %all_to_all.28 = s32[128,1,128]{2,1,0:T(1,128)} all-to-all(s32[128,1,128]{2,1,0:T(1,128)S(1)} %bitcast.27), channel_id=1, replica_groups=mesh['grp'=4,'dev'=32] {'grp','dev'}, dimensions={0} | all-to-all | bytes 131072 | tf_op jit(solution)/shard_map/all_to_all | solution.py:24
  23.9 9.2 %shard_map.177 = bf16[5120,512]{1,0:T(8,128)(2,1)} custom-call(s32[128,128]{1,0:T(8,128)} %bitcast.31, bf16[2048,512]{1,0:T(8,128)(2,1)} %refs_14_.1), custom_call_target="tpu_custom_call" | custom-call | tf_op jit(solution)/shard_map/pallas_call | solution.py:187
  33.1 0.0 copy-start.4
  33.1 0.0 copy-start.5
  33.1 5.5 %all-to-all-start.1 = ((bf16[128,40,512]{2,1,0:T(8,128)(2,1)}), bf16[128,40,512]{2,1,0:T(8,128)(2,1)}, u32[]{:S(2)}, u32[]{:S(2)}) async-start(bf16[128,40,512]{2,1,0:T(8,128)(2,1)} %bitcast.29), calls=%async_computation.1 | async-start | bytes 10485760 | tf_op jit(solution)/shard_map/all_to_all | solution.py:24
  38.7 0.1 concatenate.9
  38.8 0.1 mul.45
  38.9 0.1 slice_bitcast_fusion.1
  38.9 0.1 copy.24
  39.0 0.1 concatenate.10
  39.1 0.7 reshape.55.map_ref
  39.8 0.1 fusion
  39.9 0.7 copy.25
  40.6 0.7 reshape.62.refs_1_
  41.3 0.9 cosine_convert_fusion.2.refs_3_
  42.2 1.6 %cosine_convert_fusion.1.refs_1_ = bf16[512,128]{1,0:T(8,128)(2,1)} fusion(f32[128]{0:T(128)S(1)} %copy-done.4, f32[128]{0:T(128)S(1)} %copy-done.5, f32[512]{0:T(512)S(1)} %bitcast.38), kind=kLoop, calls=%fused_computation.1 | loop fusion | flops 196608 | bytes 134144 | tf_op jit(solution)/shard_map/convert_element_type | solution.py:492
  43.8 10.7 %cosine_convert_fusion.enc_ref = bf16[5120,128]{1,0:T(8,128)(2,1)} fusion(f32[128]{0:T(128)S(1)} %copy-done.4, f32[128]{0:T(128)S(1)} %copy-done.5, f32[5120]{0:T(1024)S(1)} %mul.45), kind=kLoop, calls=%fused_computation | loop fusion | flops 1966080 | bytes 1332224 | tf_op jit(solution)/shard_map/convert_element_type | solution.py:492
  54.5 3.8 %shard_map.178.old_ref.refs_13_ = bf16[512,512]{1,0:T(8,128)(2,1)} custom-call(s32[128,128]{1,0:T(8,128)} %bitcast.32, bf16[2048,512]{1,0:T(8,128)(2,1)} %refs_14_.1), custom_call_target="tpu_custom_call" | custom-call | tf_op jit(solution)/shard_map/pallas_call | solution.py:187
  58.3 4.3 %shard_map.180 = bf16[1024,512]{1,0:T(8,128)(2,1)} custom-call(s32[128,128]{1,0:T(8,128)} %bitcast.33, bf16[2048,512]{1,0:T(8,128)(2,1)} %refs_14_.1), custom_call_target="tpu_custom_call" | custom-call | tf_op jit(solution)/shard_map/pallas_call | solution.py:187
  62.7 0.1 slice_bitcast_fusion.2
  62.8 0.1 reshape.57.to_c_ref
  62.9 0.7 reshape.60.refs_15_
  63.6 0.1 copy.26
  63.6 3.3 %shard_map.179 = (bf16[512,512]{1,0:T(8,128)(2,1)}, f32[512,128]{1,0:T(8,128)}, bf16[512,1536]{1,0:T(8,128)(2,1)}) custom-call(s32[1,512]{1,0:T(1,128)S(1)} %reshape.57.to_c_ref, s32[1,512]{1,0:T(1,128)S(1)} %bitcast.28, bf16[512,512]{1,0:T(8,128)(2,1)} %shard_map.178.old_ref.refs_13_, bf16[512,1536]{1,0:T(8,128)(2,1)S(1)} %copy-done, f32[2,1536]{1,0:T(2,128)S(1)} %copy-done.1), custom_call_target="tpu_custom_call" | custom-call | tf_op jit(solution)/shard_map/pallas_call | solution.py:284
  66.9 36.1 %all-to-all-done.1 = bf16[128,40,512]{2,1,0:T(8,128)(2,1)} async-done(((bf16[128,40,512]{2,1,0:T(8,128)(2,1)}), bf16[128,40,512]{2,1,0:T(8,128)(2,1)}, u32[]{:S(2)}, u32[]{:S(2)}) %all-to-all-start.1) | async-done | bytes 5242912 | tf_op jit(solution)/shard_map/all_to_all | solution.py:24
  103.0 4.9 %shard_map.181 = (bf16[128,8,512]{2,1,0:T(8,128)(2,1)}, bf16[128,512]{1,0:T(8,128)(2,1)}) custom-call(bf16[128,40,512]{2,1,0:T(8,128)(2,1)} %bitcast.16.refs_0_, s32[1,1024]{1,0:T(1,128)} %reshape.62.refs_1_, bf16[1152,1024]{1,0:T(8,128)(2,1)} %refs_2_.1, bf16[128,128]{1,0:T(8,128)(2,1)} %cosine_convert_fusion.2.refs_3_, f32[1,1024]{1,0:T(1,128)} %bitcast.39, ...), custom_call_target="tpu_custom_call" | custom-call | tf_op jit(solution)/shard_map/pallas_call | solution.py:258
  108.0 6.5 %all-to-all-start.2 = ((bf16[128,8,512]{2,1,0:T(8,128)(2,1)}), bf16[128,8,512]{2,1,0:T(8,128)(2,1)S(1)}, u32[]{:S(2)}, u32[]{:S(2)}) async-start(bf16[128,8,512]{2,1,0:T(8,128)(2,1)} %get-tuple-element.31), calls=%async_computation.2 | async-start | bytes 2097152 | tf_op jit(solution)/shard_map/all_to_all | solution.py:24
  114.5 18.2 %shard_map.182 = (bf16[512,640]{1,0:T(8,128)(2,1)}, f32[512,128]{1,0:T(8,128)}, f32[512,768]{1,0:T(8,128)}) custom-call(bf16[5120,512]{1,0:T(8,128)(2,1)} %bitcast.8.rows_ref, bf16[5120,128]{1,0:T(8,128)(2,1)} %cosine_convert_fusion.enc_ref, s32[1,5120]{1,0:T(1,128)} %reshape.55.map_ref, bf16[128,512]{1,0:T(8,128)(2,1)} %get-tuple-element.36.q_ref, ...), custom_call_target="tpu_custom_call" | custom-call | tf_op jit(solution)/shard_map/pallas_call | solution.py:347
  132.6 0.8 all-to-all-done.2.refs_0_
  133.5 1.0 copy-done.2
  134.5 8.5 %shard_map.183 = (bf16[128,512]{1,0:T(8,128)(2,1)}, bf16[2048,512]{1,0:T(8,128)(2,1)}) custom-call(bf16[128,8,512]{2,1,0:T(8,128)(2,1)} %copy-done.2, bf16[512,128]{1,0:T(8,128)(2,1)} %cosine_convert_fusion.1.refs_1_, s32[1,512]{1,0:T(1,128)} %bitcast.37, bf16[512,640]{1,0:T(8,128)(2,1)} %get-tuple-element.37.refs_3_, f32[512,128]{1,0:T(8,128)} %get-tuple-element.38.refs_4_, ...), custom_call_target="tpu_custom_call" | custom-call | tf_op jit(solution)/shard_map/pallas_call | solution.py:481
  (13 shorter events, 0.0 us)
Async XLA Ops:
  33.1 5.6 %copy-start.6 = (s32[128]{0:T(128)S(1)}, s32[128]{0:T(128)}, u32[]{:S(2)}) copy-start(s32[128]{0:T(128)} %param.19) | copy-start | bytes 1540
  33.1 8.2 %copy-start.4 = (f32[128]{0:T(128)S(1)}, f32[128]{0:T(128)}, u32[]{:S(2)}) copy-start(f32[128]{0:T(128)} %param.23) | copy-start | bytes 1540
  33.1 8.2 %copy-start.5 = (f32[128]{0:T(128)S(1)}, f32[128]{0:T(128)}, u32[]{:S(2)}) copy-start(f32[128]{0:T(128)} %param.22) | copy-start | bytes 1540
  33.1 69.9 %all-to-all-start.1 = ((bf16[128,40,512]{2,1,0:T(8,128)(2,1)}), bf16[128,40,512]{2,1,0:T(8,128)(2,1)}, u32[]{:S(2)}, u32[]{:S(2)}) async-start(bf16[128,40,512]{2,1,0:T(8,128)(2,1)} %bitcast.29), calls=%async_computation.1 | async-start | bytes 10485760 | tf_op jit(solution)/shard_map/all_to_all | solution.py:24
  54.5 8.2 %copy-start.3 = (s32[128,1,128]{2,1,0:T(1,128)S(1)}, s32[128,1,128]{2,1,0:T(1,128)}, u32[]{:S(2)}) copy-start(s32[128,1,128]{2,1,0:T(1,128)} %all_to_all.28) | copy-start | bytes 196612
  58.3 5.3 %copy-start = (bf16[512,1536]{1,0:T(8,128)(2,1)S(1)}, bf16[512,1536]{1,0:T(8,128)(2,1)}, u32[]{:S(2)}) copy-start(bf16[512,1536]{1,0:T(8,128)(2,1)} %wh_ref.1) | copy-start | bytes 4718596
  58.3 5.3 %copy-start.1 = (f32[2,1536]{1,0:T(2,128)S(1)}, f32[2,1536]{1,0:T(2,128)}, u32[]{:S(2)}) copy-start(f32[2,1536]{1,0:T(2,128)} %refs_11_.1) | copy-start | bytes 36868
  108.0 25.5 %all-to-all-start.2 = ((bf16[128,8,512]{2,1,0:T(8,128)(2,1)}), bf16[128,8,512]{2,1,0:T(8,128)(2,1)S(1)}, u32[]{:S(2)}, u32[]{:S(2)}) async-start(bf16[128,8,512]{2,1,0:T(8,128)(2,1)} %get-tuple-element.31), calls=%async_computation.2 | async-start | bytes 2097152 | tf_op jit(solution)/shard_map/all_to_all | solution.py:24
  133.5 1.0 copy-start.2

commit v3 on v2

--- a/solution.py
+++ b/solution.py
@@ -9,6 +9,7 @@
 
 HDIM = 128
 LANES = 128
+PIECES = 4
 AXES = ("grp", "dev")
 F32 = jnp.float32
 BF16 = jnp.bfloat16
@@ -71,6 +72,7 @@
     acc = jnp.zeros((6 * rows, owners), F32)
     base = jnp.zeros((owners, events), F32)
     zero = jnp.zeros((1, events), jnp.int32)
+    held = []
     for k in range(fanout + 2):
         near = k < fanout
         if k == fanout:
@@ -88,7 +90,7 @@
             d = tick - nt_ref[k : k + 1, :] + 131072
             code = lane + 1
             digits = (d & 255, jnp.right_shift(d, 8) & 255, jnp.right_shift(d, 16))
-            value = local * parts
+            value = (local + 1) * parts
         else:
             slot = slot + cap_n
             code = lane + (1 + events * (k - fanout))
@@ -97,7 +99,12 @@
         vals = (value & 255, jnp.right_shift(value, 8), code) + digits
         so = srow == slot
         table = jnp.concatenate([jnp.where(so, v.astype(F32), 0.0) for v in vals], axis=0)
-        acc = acc + lax.dot_general(table.astype(BF16), ohb, NT, preferred_element_type=F32)
+        held.append((table.astype(BF16), ohb))
+        if len(held) == 2:
+            lhs = jnp.concatenate([x[0] for x in held], axis=1)
+            rhs = jnp.concatenate([x[1] for x in held], axis=1)
+            acc = acc + lax.dot_general(lhs, rhs, NT, preferred_element_type=F32)
+            held = []
     a = [acc[i * rows : (i + 1) * rows] for i in range(6)]
     pad = jnp.zeros((LANES - rows, owners), F32)
 
@@ -136,7 +143,7 @@
     return 16 // n if n < 16 else 2
 
 
-def pick_kernel(cols, shifted, req_ref, mem_ref, out_ref, req_s, mem_v, mem32, stage, out_v, sems):
+def pick_kernel(cols, static, req_ref, mem_ref, out_ref, req_s, mem_v, mem32, stage, out_v, sems):
     peers = req_ref.shape[0]
     width = mem_ref.shape[1]
     parts = width // LANES
@@ -145,57 +152,63 @@
     group = pick_group(n)
     total = n * group
     steps = peers // group // blocks
-    load_mem = pltpu.make_async_copy(mem_ref, mem_v, sems.at[0])
-    load_req = pltpu.make_async_copy(req_ref, req_s, sems.at[1])
-    load_mem.start()
+    load_req = pltpu.make_async_copy(req_ref, req_s, sems.at[0])
     load_req.start()
-    load_mem.wait()
-    spread(mem_v, mem32)
+    loads = []
+    piece = mem_ref.shape[0] // PIECES
+    for i in range(PIECES):
+        at = pl.ds(i * piece, piece)
+        loads.append(pltpu.make_async_copy(mem_ref.at[at], mem_v.at[at], sems.at[1 + i]))
+        loads[i].start()
+    mem32[0:parts, :] = jnp.zeros((parts, LANES), F32)
+    for i in range(PIECES):
+        loads[i].wait()
+        spread(mem_v.at[pl.ds(i * piece, piece)], mem32, parts + i * piece * parts)
     load_req.wait()
     copies = []
     for b in range(blocks):
 
-        def step(i, carry):
+        def step(i):
             for g in range(group):
                 o = (b * steps + i) * group + g
                 for j, col in enumerate(cols):
-                    at = req_s[o, col]
-                    if shifted[j]:
-                        at = jnp.maximum(at - parts, 0)
-                    at = pl.multiple_of(at, parts)
+                    at = pl.multiple_of(req_s[o, col], parts)
                     s = (g * n + j) * parts
                     stage[s : s + parts, :] = mem32[pl.ds(at, parts), :]
-            r = pl.multiple_of(i * total, total)
+            r = i * total if static else pl.multiple_of(i * total, total)
             gather_back(stage, 0, out_v.at[b], r, total)
-            return carry
-
-        lax.fori_loop(0, steps, step, 0)
+
+        if static:
+            for i in range(steps):
+                step(i)
+        else:
+            lax.fori_loop(0, steps, lambda i, carry: (step(i), carry)[1], 0)
         size = steps * total
-        copy = pltpu.make_async_copy(out_v.at[b], out_ref.at[pl.ds(b * size, size)], sems.at[2 + b])
+        copy = pltpu.make_async_copy(out_v.at[b], out_ref.at[pl.ds(b * size, size)], sems.at[1 + PIECES + b])
         copy.start()
         copies.append(copy)
     for copy in copies:
         copy.wait()
 
 
-def pick(req, memory, cols, shifted, blocks=4):
+def pick(req, memory, cols, static=False, blocks=4):
     peers = req.shape[0]
     nodes, width = memory.shape
     parts = width // LANES
     rows = peers * len(cols)
     anywhere = pl.BlockSpec(memory_space=pl.ANY)
     return pl.pallas_call(
-        functools.partial(pick_kernel, cols, shifted),
+        functools.partial(pick_kernel, cols, static),
         out_shape=pltpu.HBM((rows, width), BF16),
         in_specs=[anywhere, anywhere],
         out_specs=anywhere,
         scratch_shapes=[
             pltpu.SMEM(req.shape, jnp.int32),
             pltpu.VMEM((nodes, width), BF16),
-            pltpu.VMEM((nodes * parts, LANES), F32),
+            pltpu.VMEM(((nodes + 1) * parts, LANES), F32),
             pltpu.VMEM((len(cols) * pick_group(len(cols)) * parts, LANES), F32),
             pltpu.VMEM((blocks, rows // blocks, width), BF16),
-            pltpu.SemaphoreType.DMA((2 + blocks,)),
+            pltpu.SemaphoreType.DMA((1 + PIECES + blocks,)),
         ],
         compiler_params=pltpu.CompilerParams(vmem_limit_bytes=16 << 20),
     )(hbm(req), hbm(memory))
@@ -211,7 +224,7 @@
 def message_kernel(cap_e, *refs):
     ins = refs[:9]
     out_ref, q_ref = refs[9:11]
-    rows, code, w1, enc, b1, w2, b2, base, wq, out_v, q_v, sems = refs[11:]
+    rows, code, w1, enc, b1, w2, b2, base, wq, back, hidden, out_v, q_v, sems = refs[11:]
     peers, per, width = rows.shape
     slots = peers * per
     events = enc.shape[0]
@@ -220,31 +233,37 @@
     loads[1].wait()
     target = lax.broadcasted_iota(jnp.int32, (2 * events, slots), 0) + 1
     sel = jnp.where(target == code[...], 1.0, 0.0)
+    back[...] = sel.T.astype(BF16)
     loads[0].wait()
     pair = dotf(sel.astype(BF16), rows[...].reshape(slots, width)).astype(BF16)
     for i in (2, 3, 4):
         loads[i].wait()
-    first = dotf(pair, w1[:width, :])
-    second = dotf(pair, w1[width : 2 * width, :])
-    third = dotf(enc[...], w1[2 * width :, :]) + b1[...]
-    both = jnp.concatenate([second[events:] + third, second[:events] + third], axis=0)
-    hidden = jnp.maximum(first + both, 0.0).astype(BF16)
+    block = 256
+    for i in range(hidden.shape[1] // block):
+        cut = slice(i * block, (i + 1) * block)
+        second = dotf(pair, w1[width : 2 * width, cut])
+        third = dotf(enc[...], w1[2 * width :, cut]) + b1[:, cut]
+        both = jnp.concatenate([second[events:] + third, second[:events] + third], axis=0)
+        hidden[:, cut] = jnp.maximum(dotf(pair, w1[:width, cut]) + both, 0.0).astype(BF16)
     for i in (5, 6):
         loads[i].wait()
-    msg = (dotf(hidden, w2[...]) + b2[...]).astype(BF16)
-    placed = dotf(sel.T.astype(BF16), msg)
-    j = lax.broadcasted_iota(jnp.int32, (slots, width), 0) & (per - 1)
+    msg = (dotf(hidden[...], w2[...]) + b2[...]).astype(BF16)
+    j = lax.broadcasted_iota(jnp.int32, (block, width), 0) & (per - 1)
     loads[7].wait()
-    kept = base[...].reshape(slots, width).astype(F32)
-    out_v[...] = jnp.where(j < cap_e, placed, kept).astype(BF16).reshape(peers, per, width)
-    store = pltpu.make_async_copy(out_v, out_ref, sems.at[9])
-    store.start()
+    stores = []
+    for i in range(slots // block):
+        cut = slice(i * block // per, (i + 1) * block // per)
+        placed = dotf(back[i * block : (i + 1) * block, :], msg)
+        kept = base[cut].reshape(block, width).astype(F32)
+        out_v[cut] = jnp.where(j < cap_e, placed, kept).astype(BF16).reshape(block // per, per, width)
+        stores.append(pltpu.make_async_copy(out_v.at[cut], out_ref.at[cut], sems.at[9 + i]))
+        stores[i].start()
     loads[8].wait()
     q_v[...] = dotf(pair[:events], wq[...]).astype(BF16)
-    store_q = pltpu.make_async_copy(q_v, q_ref, sems.at[10])
-    store_q.start()
-    store.wait()
-    store_q.wait()
+    stores.append(pltpu.make_async_copy(q_v, q_ref, sems.at[8]))
+    stores[-1].start()
+    for store in stores:
+        store.wait()
 
 
 def messages(cap_e, got, code, w1, enc, b1, w2, b2, base, wq):
@@ -254,7 +273,13 @@
     tile = (peers, 8, width)
     anywhere = pl.BlockSpec(memory_space=pl.ANY)
     scratch = [pltpu.VMEM(tile, BF16)] + [pltpu.VMEM(x.shape, x.dtype) for x in args[1:]]
-    scratch += [pltpu.VMEM(tile, BF16), pltpu.VMEM(q_shape, BF16), pltpu.SemaphoreType.DMA((11,))]
+    scratch += [
+        pltpu.VMEM((peers * 8, 2 * q_shape[0]), BF16),
+        pltpu.VMEM((2 * q_shape[0], w1.shape[1]), BF16),
+        pltpu.VMEM(tile, BF16),
+        pltpu.VMEM(q_shape, BF16),
+        pltpu.SemaphoreType.DMA((9 + peers * 8 // 256,)),
+    ]
     return pl.pallas_call(
         functools.partial(message_kernel, cap_e),
         out_shape=(pltpu.HBM(base.shape, BF16), pltpu.HBM(q_shape, BF16)),
@@ -273,7 +298,7 @@
     hits = jnp.where(jnp.logical_and(col == tiles, tiles > 0.0), 1.0, 0.0)
     counts = jnp.sum(hits, axis=1, keepdims=True)
     hits_ref[...] = hits.astype(BF16)
-    inv_ref[...] = jnp.broadcast_to(jnp.maximum(counts, 1.0), inv_ref.shape)
+    inv_ref[...] = jnp.broadcast_to(1.0 / jnp.maximum(counts, 1.0), inv_ref.shape)
     gh_ref[...] = (dotf(old_ref[...], wh_ref[...]) + bias_ref[1:2, :]).astype(BF16)
 
 
@@ -360,24 +385,27 @@
     )(hbm(rows), hbm(enc), hbm(slot_map), hbm(query), hbm(w))
 
 
+def sigmoid(x):
+    return 0.5 * jnp.tanh(0.5 * x) + 0.5
+
+
 def finish_kernel(*refs):
-    ins = refs[:16]
+    got = refs[0]
+    ins = refs[1:16]
     emb_ref, out_ref = refs[16:18]
-    (got, enc, slot_map, qk, m_prev, a_prev, w, wo, hits, inv, wi, bias, gh, old, mem, to) = refs[18:34]
-    tile32, near, msgs, emb_v, mem32, fresh32, out_v, sems = refs[34:]
+    (enc, slot_map, qk, hits, inv, wi, bias, gh, old, m_prev, a_prev, w, wo, mem, to) = refs[18:33]
+    tile32, near, msgs, gates, emb_v, mem32, fresh32, out_v, sems = refs[33:]
     peers, per, width = got.shape
     slots = old.shape[0]
     cap = slots // peers
     nodes = mem.shape[0]
     parts = width // LANES
     blocks = out_v.shape[0]
-    inner = w.shape[0]
     heads = width // HDIM
     events = qk.shape[0] // heads
     sources = list(ins)
-    sources[6] = ins[6].at[:, pl.ds(width, width)]
-    loads = starts(list(zip(sources, refs[18:34])), sems)
-    loads[0].wait()
+    sources[11] = ins[11].at[:, pl.ds(width, width)]
+    loads = starts(list(zip(sources, refs[18:33])), sems)
     flat = got[...].reshape(peers * per, width)
     for c in range(parts):
         tile32[c] = flat[:, c * LANES : (c + 1) * LANES].astype(F32)
@@ -386,25 +414,41 @@
             for c in range(parts):
                 part = tile32[c, pl.ds(off + j, peers, stride=per), :]
                 dst[j * peers : (j + 1) * peers, c * LANES : (c + 1) * LANES] = part.astype(BF16)
-    for i in range(1, 4):
+    for i in range(5):
         loads[i].wait()
     s = block_scores(qk, near[...], enc[...], slot_map[...], events)
+    sums = dotf(hits[...], msgs[...])
     m_new = jnp.max(s, axis=1, keepdims=True)
     p = jnp.exp2(s - m_new).astype(BF16)
+    mean = (sums * inv[:, 0:1]).astype(BF16)
+    for i in (5, 6):
+        loads[i].wait()
+    gates[...] = dotf(mean, wi[...]) + bias[0:1, :]
     rows_sum, tail_sum = block_sums(p, near[...], enc[...])
-    loads[4].wait()
-    loads[5].wait()
+    for i in (7, 8):
+        loads[i].wait()
+    block = 128
+    for i in range(slots // block):
+        at = slice(i * block, (i + 1) * block)
+        r = sigmoid(gates[at, :width] + gh[at, :width].astype(F32))
+        z = sigmoid(gates[at, width : 2 * width] + gh[at, width : 2 * width].astype(F32))
+        c = jnp.tanh(gates[at, 2 * width :] + r * gh[at, 2 * width :].astype(F32))
+        fresh = (1.0 - z) * c + z * old[at, :].astype(F32)
+        for k in range(parts):
+            cut = slice(k * LANES, (k + 1) * LANES)
+            fresh32[pl.ds(i * block * parts + k, block, stride=parts), :] = fresh[:, cut]
+    for i in (9, 10, 11, 12):
+        loads[i].wait()
     before = m_prev[:, 0:1]
     m = jnp.maximum(m_new, before)
     f_new = jnp.exp2(m_new - m)
     f_old = jnp.exp2(before - m)
-    part_a = f_new * rows_sum + f_old * a_prev[:, :width]
-    part_b = f_new * tail_sum + f_old * a_prev[:, width:]
-    total = part_b[:, LANES : LANES + 1]
-    mixed_a = (part_a / total).astype(BF16)
-    mixed_b = (part_b[:, :LANES] / total).astype(BF16)
-    loads[6].wait()
-    loads[7].wait()
+    ones_at = width + LANES
+    total = f_new * tail_sum[:, LANES : LANES + 1] + f_old * a_prev[:, ones_at : ones_at + 1]
+    f_new = f_new / total
+    f_old = f_old / total
+    mixed_a = (f_new * rows_sum + f_old * a_prev[:, :width]).astype(BF16)
+    mixed_b = (f_new * tail_sum[:, :LANES] + f_old * a_prev[:, width:ones_at]).astype(BF16)
     outs = []
     for h in range(heads):
         cut = slice(h * HDIM, (h + 1) * HDIM)
@@ -412,25 +456,11 @@
         value = dotf(mixed_a[at], w[:width, cut]) + dotf(mixed_b[at], w[width:, cut])
         outs.append(value.astype(BF16))
     emb_v[...] = dotf(jnp.concatenate(outs, axis=1), wo[...]).astype(BF16)
-    copies = [pltpu.make_async_copy(emb_v, emb_ref, sems.at[16])]
+    copies = [pltpu.make_async_copy(emb_v, emb_ref, sems.at[15])]
     copies[0].start()
-
-    for i in range(8, 12):
-        loads[i].wait()
-    sums = dotf(hits[...], msgs[...])
-    mean = (sums / inv[:, 0:1]).astype(BF16)
-    gi = dotf(mean, wi[...]) + bias[0:1, :]
-    loads[12].wait()
     loads[13].wait()
-    r = jax.nn.sigmoid(gi[:, :width] + gh[:, :width].astype(F32))
-    z = jax.nn.sigmoid(gi[:, width : 2 * width] + gh[:, width : 2 * width].astype(F32))
-    c = jnp.tanh(gi[:, 2 * width :] + r * gh[:, 2 * width :].astype(F32))
-    fresh = (1.0 - z) * c + z * old[...].astype(F32)
-    for k in range(parts):
-        fresh32[pl.ds(k, slots, stride=parts), :] = fresh[:, k * LANES : (k + 1) * LANES]
+    spread(mem, mem32, parts)
     loads[14].wait()
-    spread(mem, mem32, parts)
-    loads[15].wait()
 
     def step(i, carry):
         for k in range(16):
@@ -449,15 +479,15 @@
             return carry
 
         lax.fori_loop(0, size // 128, back, 0)
-        copy = pltpu.make_async_copy(out_v.at[b], out_ref.at[pl.ds(b * size, size)], sems.at[17 + b])
+        copy = pltpu.make_async_copy(out_v.at[b], out_ref.at[pl.ds(b * size, size)], sems.at[16 + b])
         copy.start()
         copies.append(copy)
     for copy in copies:
         copy.wait()
 
 
-def finish(got, enc, slot_map, qk, m, a, w, wo, hits, inv, wi, bias, gh, old, memory, to, blocks=4):
-    args = (got, enc, slot_map, qk, m, a, w, wo, hits, inv, wi, bias, gh, old, memory, to)
+def finish(got, enc, slot_map, qk, hits, inv, wi, bias, gh, old, m, a, w, wo, memory, to, blocks=4):
+    args = (enc, slot_map, qk, hits, inv, wi, bias, gh, old, m, a, w, wo, memory, to)
     peers, per, width = got.shape
     nodes = memory.shape[0]
     slots = old.shape[0]
@@ -465,27 +495,28 @@
     emb_shape = (qk.shape[0] // (width // HDIM), width)
     anywhere = pl.BlockSpec(memory_space=pl.ANY)
     shapes = [x.shape for x in args[:-1]]
-    shapes[6] = (w.shape[0], width)
+    shapes[11] = (w.shape[0], width)
     scratch = [pltpu.VMEM(shape, x.dtype) for shape, x in zip(shapes, args)]
     scratch += [
         pltpu.SMEM(to.shape, jnp.int32),
         pltpu.VMEM((parts, peers * per, LANES), F32),
         pltpu.VMEM((slots, width), BF16),
         pltpu.VMEM((slots, width), BF16),
+        pltpu.VMEM((slots, wi.shape[1]), F32),
         pltpu.VMEM(emb_shape, BF16),
         pltpu.VMEM(((nodes + 1) * parts, LANES), F32),
         pltpu.VMEM((slots * parts, LANES), F32),
         pltpu.VMEM((blocks, nodes // blocks, width), BF16),
-        pltpu.SemaphoreType.DMA((17 + blocks,)),
+        pltpu.SemaphoreType.DMA((16 + blocks,)),
     ]
     return pl.pallas_call(
         finish_kernel,
         out_shape=(pltpu.HBM(emb_shape, BF16), pltpu.HBM(memory.shape, BF16)),
-        in_specs=[anywhere] * len(args),
+        in_specs=[pl.BlockSpec(memory_space=pltpu.VMEM)] + [anywhere] * len(args),
         out_specs=(anywhere, anywhere),
         scratch_shapes=scratch,
         compiler_params=pltpu.CompilerParams(vmem_limit_bytes=44 << 20),
-    )(*[hbm(x) for x in args])
+    )(got, *[hbm(x) for x in args])
 
 
 def encode(dt, freq, phase):
@@ -537,10 +568,10 @@
     cols_a = ev + tuple(range(near))
     cols_c = tuple(range(near, near + cap_e)) + tuple(range(near, cap_n))
     take = functools.partial(pick, asked, memory)
-    sent_a = take(cols_a, (True,) * cap_e + (False,) * near)
+    sent_a = take(cols_a, static=True, blocks=8)
     got_a = exchange(sent_a)
-    base_c = take(cols_c, (False,) * len(cols_c)).reshape(owners, -1, width)
-    old = take(ev, (True,) * cap_e)
+    base_c = take(cols_c).reshape(owners, -1, width)
+    old = take(ev)
 
     def spaced(x):
         return jnp.concatenate([jnp.zeros((owners, cap_e), x.dtype), x], axis=1)
@@ -553,12 +584,12 @@
     map_c = owner_map[:, near:cap_n].T.reshape(1, -1)
     to = asked[:, cap_n : cap_n + cap_e]
     to_s = to.reshape(-1)
-    hits, counts, gh = prepare(to.reshape(1, -1), to.T.reshape(1, -1), old, gru_hidden, gru_bias)
+    hits, inv, gh = prepare(to.reshape(1, -1), to.T.reshape(1, -1), old, gru_hidden, gru_bias)
     enc_a = encode(spaced(dt[:, :near]), freq, phase).reshape(-1, LANES)
     enc_c = encode(dt[:, near:cap_n].T, freq, phase).reshape(-1, LANES)
     enc = encode(event_ticks.astype(F32), freq, phase)
-    got_a, enc_a, enc_c, map_a, map_c, hits, counts, gh, base_c, to_s = lax.optimization_barrier(
-        (got_a, enc_a, enc_c, map_a, map_c, hits, counts, gh, base_c, to_s)
+    got_a, enc_a, enc_c, map_a, map_c, hits, inv, gh, base_c, to_s = lax.optimization_barrier(
+        (got_a, enc_a, enc_c, map_a, map_c, hits, inv, gh, base_c, to_s)
     )
     sent_c, query = messages(
         cap_e,
@@ -579,16 +610,16 @@
         enc_c,
         map_c,
         qk,
+        hits,
+        inv,
+        gru_input,
+        gru_bias,
+        gh,
+        old,
         m,
         a,
         w_keyval,
         w_out,
-        hits,
-        counts,
-        gru_input,
-        gru_bias,
-        gh,
-        old,
         memory,
         to_s,
     )

time: 144 us -> 139 us (0.965)
  Pallas kernels: 54.4 us -> 50.5 us
    pallas_call x3, Pallas kernels: 17.3 us -> 14.4 us  [pick(): pl.pallas_call(functools.partial(pick_kernel, cols, static), out_shape=pl...]
where the time goes in v3:
time: 139 us
  Pallas kernels  50.5 us (36%)
  waiting for transfers between devices  37.7 us (27%)
  blocking collectives  21.1 us (15%)
  other arithmetic  13.1 us (9%)
  starting transfers between devices  11.8 us (8%)
  local copies, waits for them, and re-layouts  3.57 us (3%)
    all_to_all x2, waiting for transfers between devices, exchange(): return lax.all_to_all(x, AXES, split_axis=0, concat_axis=0, tiled=True)  37.7 us
    all_to_all x1, blocking collectives, exchange(): return lax.all_to_all(x, AXES, split_axis=0, concat_axis=0, tiled=True)  21.1 us
    pallas_call x1, Pallas kernels, attend(): pl.pallas_call(attend_kernel, out_shape=tuple((pltpu.HBM(*x) for x in sha...  18.2 us
    pallas_call x3, Pallas kernels, pick(): pl.pallas_call(functools.partial(pick_kernel, cols, static), out_shape=pl...  14.4 us
    convert_element_type x3, other arithmetic, encode(): return jnp.cos(dt[..., None] * freq + phase).astype(BF16)  13.1 us
    all_to_all x2, starting transfers between devices, exchange(): return lax.all_to_all(x, AXES, split_axis=0, concat_axis=0, tiled=True)  11.8 us
    pallas_call x1, Pallas kernels, finish(): pl.pallas_call(finish_kernel, out_shape=(pltpu.HBM(emb_shape, BF16), pltp...  7.74 us
    pallas_call x1, Pallas kernels, messages(): pl.pallas_call(functools.partial(message_kernel, cap_e), out_shape=(pltpu...  4.79 us
  transfers between devices with their start and end apart: 2, of which 2 were waited for; matrix products, arithmetic and copies ran while one was open for 12% of the time, Pallas kernels for 21%

profile of v3, /device:TPU:1, one launch (start us, length us, event | category | flops | bytes accessed | tf_op | source)
XLA Modules:
  0.0 138.9 jit_solution(8484275245611713061)
XLA Ops:
  0.6 2.2 %shard_map.176 = (s32[128,128]{1,0:T(8,128)S(1)}, s32[128,128]{1,0:T(8,128)S(1)}, f32[128,128]{1,0:T(8,128)S(1)}) custom-call(s32[20,128]{1,0:T(8,128)} %bitcast.35, s32[20,128]{1,0:T(8,128)} %bitcast.36, s32[2,128]{1,0:T(2,128)} %bitcast.41, s32[1,128]{1,0:T(1,128)} %bitcast.42), custom_call_target="tpu_custom_call" | custom-call | tf_op jit(solution)/shard_map/pallas_call | solution.py:29
  2.8 21.1 %all_to_all.28 = s32[128,1,128]{2,1,0:T(1,128)} all-to-all(s32[128,1,128]{2,1,0:T(1,128)S(1)} %bitcast.27), channel_id=1, replica_groups=mesh['grp'=4,'dev'=32] {'grp','dev'}, dimensions={0} | all-to-all | bytes 131072 | tf_op jit(solution)/shard_map/all_to_all | solution.py:25
  23.9 7.0 %shard_map.177 = bf16[5120,512]{1,0:T(8,128)(2,1)} custom-call(s32[128,128]{1,0:T(8,128)} %bitcast.31, bf16[2048,512]{1,0:T(8,128)(2,1)} %refs_14_.1), custom_call_target="tpu_custom_call" | custom-call | tf_op jit(solution)/shard_map/pallas_call | solution.py:200
  30.9 0.0 copy-start.5
  30.9 0.0 copy-start.3
  30.9 0.0 copy-start.4
  30.9 5.7 %all-to-all-start.1 = ((bf16[128,40,512]{2,1,0:T(8,128)(2,1)}), bf16[128,40,512]{2,1,0:T(8,128)(2,1)}, u32[]{:S(2)}, u32[]{:S(2)}) async-start(bf16[128,40,512]{2,1,0:T(8,128)(2,1)} %bitcast.29), calls=%async_computation.1 | async-start | bytes 10485760 | tf_op jit(solution)/shard_map/all_to_all | solution.py:25
  36.6 0.1 concatenate.9
  36.7 0.1 mul.45
  36.8 0.1 slice_bitcast_fusion.1
  36.9 0.1 copy.24
  36.9 0.1 concatenate.10
  37.0 0.7 reshape.55.map_ref
  37.8 0.1 fusion
  37.9 0.7 copy.25
  38.5 0.7 reshape.62.refs_1_
  39.2 0.9 cosine_convert_fusion.2.refs_3_
  40.1 1.6 %cosine_convert_fusion.1.refs_1_ = bf16[512,128]{1,0:T(8,128)(2,1)} fusion(f32[128]{0:T(128)S(1)} %copy-done.3, f32[128]{0:T(128)S(1)} %copy-done.4, f32[512]{0:T(512)S(1)} %bitcast.38), kind=kLoop, calls=%fused_computation.1 | loop fusion | flops 196608 | bytes 134144 | tf_op jit(solution)/shard_map/convert_element_type | solution.py:523
  41.7 10.7 %cosine_convert_fusion.enc_ref = bf16[5120,128]{1,0:T(8,128)(2,1)} fusion(f32[128]{0:T(128)S(1)} %copy-done.3, f32[128]{0:T(128)S(1)} %copy-done.4, f32[5120]{0:T(1024)S(1)} %mul.45), kind=kLoop, calls=%fused_computation | loop fusion | flops 1966080 | bytes 1332224 | tf_op jit(solution)/shard_map/convert_element_type | solution.py:523
  52.4 3.3 %shard_map.178.old_ref.refs_9_ = bf16[512,512]{1,0:T(8,128)(2,1)} custom-call(s32[128,128]{1,0:T(8,128)} %bitcast.32, bf16[2048,512]{1,0:T(8,128)(2,1)} %refs_14_.1), custom_call_target="tpu_custom_call" | custom-call | tf_op jit(solution)/shard_map/pallas_call | solution.py:200
  55.7 4.1 %shard_map.180 = bf16[1024,512]{1,0:T(8,128)(2,1)} custom-call(s32[128,128]{1,0:T(8,128)} %bitcast.33, bf16[2048,512]{1,0:T(8,128)(2,1)} %refs_14_.1), custom_call_target="tpu_custom_call" | custom-call | tf_op jit(solution)/shard_map/pallas_call | solution.py:200
  59.8 0.1 slice_bitcast_fusion.2
  59.9 0.1 reshape.57.to_c_ref
  60.0 0.7 reshape.60.refs_15_
  60.7 0.1 copy.26
  60.8 3.3 %shard_map.179 = (bf16[512,512]{1,0:T(8,128)(2,1)}, f32[512,128]{1,0:T(8,128)}, bf16[512,1536]{1,0:T(8,128)(2,1)}) custom-call(s32[1,512]{1,0:T(1,128)S(1)} %reshape.57.to_c_ref, s32[1,512]{1,0:T(1,128)S(1)} %bitcast.28, bf16[512,512]{1,0:T(8,128)(2,1)} %shard_map.178.old_ref.refs_9_, bf16[512,1536]{1,0:T(8,128)(2,1)S(1)} %copy-done, f32[2,1536]{1,0:T(2,128)S(1)} %copy-done.1), custom_call_target="tpu_custom_call" | custom-call | tf_op jit(solution)/shard_map/pallas_call | solution.py:309
  64.1 36.9 %all-to-all-done.1 = bf16[128,40,512]{2,1,0:T(8,128)(2,1)} async-done(((bf16[128,40,512]{2,1,0:T(8,128)(2,1)}), bf16[128,40,512]{2,1,0:T(8,128)(2,1)}, u32[]{:S(2)}, u32[]{:S(2)}) %all-to-all-start.1) | async-done | bytes 5242912 | tf_op jit(solution)/shard_map/all_to_all | solution.py:25
  100.9 4.8 %shard_map.181 = (bf16[128,8,512]{2,1,0:T(8,128)(2,1)}, bf16[128,512]{1,0:T(8,128)(2,1)}) custom-call(bf16[128,40,512]{2,1,0:T(8,128)(2,1)} %bitcast.16.refs_0_, s32[1,1024]{1,0:T(1,128)} %reshape.62.refs_1_, bf16[1152,1024]{1,0:T(8,128)(2,1)} %refs_2_.1, bf16[128,128]{1,0:T(8,128)(2,1)} %cosine_convert_fusion.2.refs_3_, f32[1,1024]{1,0:T(1,128)} %bitcast.39, ...), custom_call_target="tpu_custom_call" | custom-call | tf_op jit(solution)/shard_map/pallas_call | solution.py:283
  105.7 6.2 %all-to-all-start.2 = ((bf16[128,8,512]{2,1,0:T(8,128)(2,1)}), bf16[128,8,512]{2,1,0:T(8,128)(2,1)S(1)}, u32[]{:S(2)}, u32[]{:S(2)}) async-start(bf16[128,8,512]{2,1,0:T(8,128)(2,1)} %get-tuple-element.31), calls=%async_computation.2 | async-start | bytes 2097152 | tf_op jit(solution)/shard_map/all_to_all | solution.py:25
  111.9 18.2 %shard_map.182 = (bf16[512,640]{1,0:T(8,128)(2,1)}, f32[512,128]{1,0:T(8,128)}, f32[512,768]{1,0:T(8,128)}) custom-call(bf16[5120,512]{1,0:T(8,128)(2,1)} %bitcast.8.rows_ref, bf16[5120,128]{1,0:T(8,128)(2,1)} %cosine_convert_fusion.enc_ref, s32[1,5120]{1,0:T(1,128)} %reshape.55.map_ref, bf16[128,512]{1,0:T(8,128)(2,1)} %get-tuple-element.36.q_ref, ...), custom_call_target="tpu_custom_call" | custom-call | tf_op jit(solution)/shard_map/pallas_call | solution.py:372
  130.1 0.8 all-to-all-done.2.refs_0_
  130.9 7.7 %shard_map.183 = (bf16[128,512]{1,0:T(8,128)(2,1)}, bf16[2048,512]{1,0:T(8,128)(2,1)}) custom-call(bf16[128,8,512]{2,1,0:T(8,128)(2,1)S(1)} %all-to-all-done.2.refs_0_, bf16[512,128]{1,0:T(8,128)(2,1)} %cosine_convert_fusion.1.refs_1_, s32[1,512]{1,0:T(1,128)} %bitcast.37, bf16[512,640]{1,0:T(8,128)(2,1)} %get-tuple-element.37.refs_3_, ...), custom_call_target="tpu_custom_call" | custom-call | tf_op jit(solution)/shard_map/pallas_call | solution.py:512
  (11 shorter events, 0.0 us)
Async XLA Ops:
  30.9 5.7 %copy-start.5 = (s32[128]{0:T(128)S(1)}, s32[128]{0:T(128)}, u32[]{:S(2)}) copy-start(s32[128]{0:T(128)} %param.19) | copy-start | bytes 1540
  30.9 8.3 %copy-start.3 = (f32[128]{0:T(128)S(1)}, f32[128]{0:T(128)}, u32[]{:S(2)}) copy-start(f32[128]{0:T(128)} %param.23) | copy-start | bytes 1540
  30.9 8.3 %copy-start.4 = (f32[128]{0:T(128)S(1)}, f32[128]{0:T(128)}, u32[]{:S(2)}) copy-start(f32[128]{0:T(128)} %param.22) | copy-start | bytes 1540
  30.9 70.0 %all-to-all-start.1 = ((bf16[128,40,512]{2,1,0:T(8,128)(2,1)}), bf16[128,40,512]{2,1,0:T(8,128)(2,1)}, u32[]{:S(2)}, u32[]{:S(2)}) async-start(bf16[128,40,512]{2,1,0:T(8,128)(2,1)} %bitcast.29), calls=%async_computation.1 | async-start | bytes 10485760 | tf_op jit(solution)/shard_map/all_to_all | solution.py:25
  52.4 7.5 %copy-start.2 = (s32[128,1,128]{2,1,0:T(1,128)S(1)}, s32[128,1,128]{2,1,0:T(1,128)}, u32[]{:S(2)}) copy-start(s32[128,1,128]{2,1,0:T(1,128)} %all_to_all.28) | copy-start | bytes 196612
  55.7 5.1 %copy-start = (bf16[512,1536]{1,0:T(8,128)(2,1)S(1)}, bf16[512,1536]{1,0:T(8,128)(2,1)}, u32[]{:S(2)}) copy-start(bf16[512,1536]{1,0:T(8,128)(2,1)} %wh_ref.1) | copy-start | bytes 4718596
  55.7 5.1 %copy-start.1 = (f32[2,1536]{1,0:T(2,128)S(1)}, f32[2,1536]{1,0:T(2,128)}, u32[]{:S(2)}) copy-start(f32[2,1536]{1,0:T(2,128)} %refs_7_.1) | copy-start | bytes 36868
  105.7 25.2 %all-to-all-start.2 = ((bf16[128,8,512]{2,1,0:T(8,128)(2,1)}), bf16[128,8,512]{2,1,0:T(8,128)(2,1)S(1)}, u32[]{:S(2)}, u32[]{:S(2)}) async-start(bf16[128,8,512]{2,1,0:T(8,128)(2,1)} %get-tuple-element.31), calls=%async_computation.2 | async-start | bytes 2097152 | tf_op jit(solution)/shard_map/all_to_all | solution.py:25

commit v4 on v3

--- a/solution.py
+++ b/solution.py
@@ -117,19 +117,25 @@
     dt_ref[...] = turned(jnp.where(a[2] > 0.0, dt, 0.0))
 
 
-def spread(src_ref, dst_ref, base=0):
+def spread(src_ref, dst_ref, base=0, static=False):
     rows, width = src_ref.shape
     parts = width // LANES
     block = 128
 
-    def step(i, carry):
-        r = pl.multiple_of(i * block, block)
+    def step(r):
         for c in range(parts):
             part = src_ref[pl.ds(r, block), c * LANES : (c + 1) * LANES].astype(F32)
             dst_ref[pl.ds(base + r * parts + c, block, stride=parts), :] = part
+
+    def turn(i, carry):
+        step(pl.multiple_of(i * block, block))
         return carry
 
-    lax.fori_loop(0, rows // block, step, 0)
+    if static:
+        for i in range(rows // block):
+            step(i * block)
+    else:
+        lax.fori_loop(0, rows // block, turn, 0)
 
 
 def gather_back(src_ref, base, dst_ref, row, rows):
@@ -222,21 +228,22 @@
 
 
 def message_kernel(cap_e, *refs):
-    ins = refs[:9]
+    w1 = refs[0]
+    ins = refs[1:9]
     out_ref, q_ref = refs[9:11]
-    rows, code, w1, enc, b1, w2, b2, base, wq, back, hidden, out_v, q_v, sems = refs[11:]
+    rows, code, enc, b1, w2, b2, base, wq, back, hidden, out_v, q_v, sems = refs[11:]
     peers, per, width = rows.shape
     slots = peers * per
     events = enc.shape[0]
     sources = (ins[0].at[:, 0:per, :],) + tuple(ins[1:])
-    loads = starts(list(zip(sources, (rows, code, w1, enc, b1, w2, b2, base, wq))), sems)
+    loads = starts(list(zip(sources, (rows, code, enc, b1, w2, b2, base, wq))), sems)
     loads[1].wait()
     target = lax.broadcasted_iota(jnp.int32, (2 * events, slots), 0) + 1
     sel = jnp.where(target == code[...], 1.0, 0.0)
     back[...] = sel.T.astype(BF16)
     loads[0].wait()
     pair = dotf(sel.astype(BF16), rows[...].reshape(slots, width)).astype(BF16)
-    for i in (2, 3, 4):
+    for i in (2, 3):
         loads[i].wait()
     block = 256
     for i in range(hidden.shape[1] // block):
@@ -245,22 +252,22 @@
         third = dotf(enc[...], w1[2 * width :, cut]) + b1[:, cut]
         both = jnp.concatenate([second[events:] + third, second[:events] + third], axis=0)
         hidden[:, cut] = jnp.maximum(dotf(pair, w1[:width, cut]) + both, 0.0).astype(BF16)
-    for i in (5, 6):
+    for i in (4, 5):
         loads[i].wait()
     msg = (dotf(hidden[...], w2[...]) + b2[...]).astype(BF16)
     j = lax.broadcasted_iota(jnp.int32, (block, width), 0) & (per - 1)
-    loads[7].wait()
+    loads[6].wait()
     stores = []
     for i in range(slots // block):
         cut = slice(i * block // per, (i + 1) * block // per)
         placed = dotf(back[i * block : (i + 1) * block, :], msg)
         kept = base[cut].reshape(block, width).astype(F32)
         out_v[cut] = jnp.where(j < cap_e, placed, kept).astype(BF16).reshape(block // per, per, width)
-        stores.append(pltpu.make_async_copy(out_v.at[cut], out_ref.at[cut], sems.at[9 + i]))
+        stores.append(pltpu.make_async_copy(out_v.at[cut], out_ref.at[cut], sems.at[8 + i]))
         stores[i].start()
-    loads[8].wait()
+    loads[7].wait()
     q_v[...] = dotf(pair[:events], wq[...]).astype(BF16)
-    stores.append(pltpu.make_async_copy(q_v, q_ref, sems.at[8]))
+    stores.append(pltpu.make_async_copy(q_v, q_ref, sems.at[7]))
     stores[-1].start()
     for store in stores:
         store.wait()
@@ -268,7 +275,7 @@
 
 def messages(cap_e, got, code, w1, enc, b1, w2, b2, base, wq):
     peers, _, width = got.shape
-    args = (got, code, w1, enc, b1, w2, b2, base, wq)
+    args = (got, code, enc, b1, w2, b2, base, wq)
     q_shape = (enc.shape[0], width)
     tile = (peers, 8, width)
     anywhere = pl.BlockSpec(memory_space=pl.ANY)
@@ -283,36 +290,27 @@
     return pl.pallas_call(
         functools.partial(message_kernel, cap_e),
         out_shape=(pltpu.HBM(base.shape, BF16), pltpu.HBM(q_shape, BF16)),
-        in_specs=[anywhere] * len(args),
+        in_specs=[pl.BlockSpec(memory_space=pltpu.VMEM)] + [anywhere] * len(args),
         out_specs=(anywhere, anywhere),
         scratch_shapes=scratch,
         compiler_params=pltpu.CompilerParams(vmem_limit_bytes=28 << 20),
-    )(*[hbm(x) for x in args])
-
-
-def prepare_kernel(to_c_ref, to_t_ref, old_ref, wh_ref, bias_ref, hits_ref, inv_ref, gh_ref):
-    slots = old_ref.shape[0]
-    row = to_c_ref[...].astype(F32)
-    col = jnp.broadcast_to(row, (8, slots)).T[:, 0:1]
-    tiles = to_t_ref[...].astype(F32)
-    hits = jnp.where(jnp.logical_and(col == tiles, tiles > 0.0), 1.0, 0.0)
-    counts = jnp.sum(hits, axis=1, keepdims=True)
-    hits_ref[...] = hits.astype(BF16)
-    inv_ref[...] = jnp.broadcast_to(1.0 / jnp.maximum(counts, 1.0), inv_ref.shape)
+    )(w1, *[hbm(x) for x in args])
+
+
+def prepare_kernel(old_ref, wh_ref, bias_ref, gh_ref):
     gh_ref[...] = (dotf(old_ref[...], wh_ref[...]) + bias_ref[1:2, :]).astype(BF16)
 
 
-def prepare(to_c, to_t, old, wh, bias):
-    slots = old.shape[0]
-    args = (to_c, to_t, hbm(old), wh, bias)
-    out = ((slots, to_t.shape[1]), BF16), ((slots, LANES), F32), ((slots, wh.shape[1]), BF16)
+def prepare(old, wh, bias):
+    args = (hbm(old), hbm(wh), hbm(bias))
+    shape = (old.shape[0], wh.shape[1])
     return pl.pallas_call(
         prepare_kernel,
-        out_shape=tuple(pltpu.HBM(*x) for x in out),
+        out_shape=pltpu.HBM(shape, BF16),
         grid=(1,),
         in_specs=[whole(x) for x in args],
-        out_specs=tuple(whole(sds(*x)) for x in out),
-        compiler_params=pltpu.CompilerParams(vmem_limit_bytes=24 << 20),
+        out_specs=whole(sds(shape, BF16)),
+        compiler_params=pltpu.CompilerParams(vmem_limit_bytes=16 << 20),
     )(*args)
 
 
@@ -371,7 +369,7 @@
     )
     return pl.pallas_call(
         attend_kernel,
-        out_shape=tuple(pltpu.HBM(*x) for x in shapes),
+        out_shape=tuple(pltpu.VMEM(*x) for x in shapes),
         grid=(total // block,),
         in_specs=[
             pl.BlockSpec((block, width), lambda i: (i, 0)),
@@ -390,11 +388,11 @@
 
 
 def finish_kernel(*refs):
-    got = refs[0]
-    ins = refs[1:16]
+    got, qk, m_prev, a_prev = refs[:4]
+    ins = refs[4:16]
     emb_ref, out_ref = refs[16:18]
-    (enc, slot_map, qk, hits, inv, wi, bias, gh, old, m_prev, a_prev, w, wo, mem, to) = refs[18:33]
-    tile32, near, msgs, gates, emb_v, mem32, fresh32, out_v, sems = refs[33:]
+    (enc, slot_map, to_c, to_t, wi, bias, gh, old, mem, w, wo, to) = refs[18:30]
+    tile32, near, gates, emb_v, mem32, fresh32, out_v, sems = refs[30:]
     peers, per, width = got.shape
     slots = old.shape[0]
     cap = slots // peers
@@ -404,29 +402,31 @@
     heads = width // HDIM
     events = qk.shape[0] // heads
     sources = list(ins)
-    sources[11] = ins[11].at[:, pl.ds(width, width)]
-    loads = starts(list(zip(sources, refs[18:33])), sems)
+    sources[9] = ins[9].at[:, pl.ds(width, width)]
+    loads = starts(list(zip(sources, refs[18:30])), sems)
     flat = got[...].reshape(peers * per, width)
     for c in range(parts):
         tile32[c] = flat[:, c * LANES : (c + 1) * LANES].astype(F32)
-    for dst, off in ((near, cap), (msgs, 0)):
-        for j in range(cap):
-            for c in range(parts):
-                part = tile32[c, pl.ds(off + j, peers, stride=per), :]
-                dst[j * peers : (j + 1) * peers, c * LANES : (c + 1) * LANES] = part.astype(BF16)
-    for i in range(5):
+    for j in range(cap):
+        for c in range(parts):
+            part = tile32[c, pl.ds(per - cap + j, peers, stride=per), :]
+            near[j * peers : (j + 1) * peers, c * LANES : (c + 1) * LANES] = part.astype(BF16)
+    for i in range(4):
         loads[i].wait()
     s = block_scores(qk, near[...], enc[...], slot_map[...], events)
-    sums = dotf(hits[...], msgs[...])
+    col = jnp.broadcast_to(to_c[...].astype(F32), (8, slots)).T[:, 0:1]
+    tiles = to_t[...].astype(F32)
+    hits = jnp.where(jnp.logical_and(col == tiles, tiles > 0.0), 1.0, 0.0)
+    counts = jnp.sum(hits, axis=1, keepdims=True)
+    sums = dotf(hits.astype(BF16), flat)
     m_new = jnp.max(s, axis=1, keepdims=True)
     p = jnp.exp2(s - m_new).astype(BF16)
-    mean = (sums * inv[:, 0:1]).astype(BF16)
-    for i in (5, 6):
+    mean = (sums * (1.0 / jnp.maximum(counts, 1.0))).astype(BF16)
+    for i in range(4, 9):
         loads[i].wait()
     gates[...] = dotf(mean, wi[...]) + bias[0:1, :]
+    spread(mem, mem32, parts, static=True)
     rows_sum, tail_sum = block_sums(p, near[...], enc[...])
-    for i in (7, 8):
-        loads[i].wait()
     block = 128
     for i in range(slots // block):
         at = slice(i * block, (i + 1) * block)
@@ -437,7 +437,7 @@
         for k in range(parts):
             cut = slice(k * LANES, (k + 1) * LANES)
             fresh32[pl.ds(i * block * parts + k, block, stride=parts), :] = fresh[:, cut]
-    for i in (9, 10, 11, 12):
+    for i in range(9, 12):
         loads[i].wait()
     before = m_prev[:, 0:1]
     m = jnp.maximum(m_new, before)
@@ -456,20 +456,11 @@
         value = dotf(mixed_a[at], w[:width, cut]) + dotf(mixed_b[at], w[width:, cut])
         outs.append(value.astype(BF16))
     emb_v[...] = dotf(jnp.concatenate(outs, axis=1), wo[...]).astype(BF16)
-    copies = [pltpu.make_async_copy(emb_v, emb_ref, sems.at[15])]
+    copies = [pltpu.make_async_copy(emb_v, emb_ref, sems.at[12])]
     copies[0].start()
-    loads[13].wait()
-    spread(mem, mem32, parts)
-    loads[14].wait()
-
-    def step(i, carry):
-        for k in range(16):
-            s = i * 16 + k
-            at = pl.multiple_of(to[s], parts)
-            mem32[pl.ds(at, parts), :] = fresh32[pl.ds(pl.multiple_of(s * parts, parts), parts), :]
-        return carry
-
-    lax.fori_loop(0, slots // 16, step, 0)
+    for s in range(slots):
+        at = pl.multiple_of(to[s], parts)
+        mem32[pl.ds(at, parts), :] = fresh32[s * parts : (s + 1) * parts, :]
     size = nodes // blocks
     for b in range(blocks):
 
@@ -479,15 +470,15 @@
             return carry
 
         lax.fori_loop(0, size // 128, back, 0)
-        copy = pltpu.make_async_copy(out_v.at[b], out_ref.at[pl.ds(b * size, size)], sems.at[16 + b])
+        copy = pltpu.make_async_copy(out_v.at[b], out_ref.at[pl.ds(b * size, size)], sems.at[13 + b])
         copy.start()
         copies.append(copy)
     for copy in copies:
         copy.wait()
 
 
-def finish(got, enc, slot_map, qk, hits, inv, wi, bias, gh, old, m, a, w, wo, memory, to, blocks=4):
-    args = (enc, slot_map, qk, hits, inv, wi, bias, gh, old, m, a, w, wo, memory, to)
+def finish(got, qk, m, a, enc, slot_map, to_c, to_t, wi, bias, gh, old, memory, w, wo, to, blocks=4):
+    args = (enc, slot_map, to_c, to_t, wi, bias, gh, old, memory, w, wo, to)
     peers, per, width = got.shape
     nodes = memory.shape[0]
     slots = old.shape[0]
@@ -495,28 +486,27 @@
     emb_shape = (qk.shape[0] // (width // HDIM), width)
     anywhere = pl.BlockSpec(memory_space=pl.ANY)
     shapes = [x.shape for x in args[:-1]]
-    shapes[11] = (w.shape[0], width)
+    shapes[9] = (w.shape[0], width)
     scratch = [pltpu.VMEM(shape, x.dtype) for shape, x in zip(shapes, args)]
     scratch += [
         pltpu.SMEM(to.shape, jnp.int32),
         pltpu.VMEM((parts, peers * per, LANES), F32),
-        pltpu.VMEM((slots, width), BF16),
         pltpu.VMEM((slots, width), BF16),
         pltpu.VMEM((slots, wi.shape[1]), F32),
         pltpu.VMEM(emb_shape, BF16),
         pltpu.VMEM(((nodes + 1) * parts, LANES), F32),
         pltpu.VMEM((slots * parts, LANES), F32),
         pltpu.VMEM((blocks, nodes // blocks, width), BF16),
-        pltpu.SemaphoreType.DMA((16 + blocks,)),
+        pltpu.SemaphoreType.DMA((13 + blocks,)),
     ]
     return pl.pallas_call(
         finish_kernel,
         out_shape=(pltpu.HBM(emb_shape, BF16), pltpu.HBM(memory.shape, BF16)),
-        in_specs=[pl.BlockSpec(memory_space=pltpu.VMEM)] + [anywhere] * len(args),
+        in_specs=[pl.BlockSpec(memory_space=pltpu.VMEM)] * 4 + [anywhere] * len(args),
         out_specs=(anywhere, anywhere),
         scratch_shapes=scratch,
         compiler_params=pltpu.CompilerParams(vmem_limit_bytes=44 << 20),
-    )(got, *[hbm(x) for x in args])
+    )(got, vmem(qk), vmem(m), vmem(a), *[hbm(x) for x in args])
 
 
 def encode(dt, freq, phase):
@@ -584,12 +574,14 @@
     map_c = owner_map[:, near:cap_n].T.reshape(1, -1)
     to = asked[:, cap_n : cap_n + cap_e]
     to_s = to.reshape(-1)
-    hits, inv, gh = prepare(to.reshape(1, -1), to.T.reshape(1, -1), old, gru_hidden, gru_bias)
+    to_c = to.reshape(1, -1)
+    to_t = tiled(to)
+    gh = prepare(old, gru_hidden, gru_bias)
     enc_a = encode(spaced(dt[:, :near]), freq, phase).reshape(-1, LANES)
     enc_c = encode(dt[:, near:cap_n].T, freq, phase).reshape(-1, LANES)
     enc = encode(event_ticks.astype(F32), freq, phase)
-    got_a, enc_a, enc_c, map_a, map_c, hits, inv, gh, base_c, to_s = lax.optimization_barrier(
-        (got_a, enc_a, enc_c, map_a, map_c, hits, inv, gh, base_c, to_s)
+    got_a, enc_a, enc_c, map_a, map_c, to_c, to_t, gh, base_c, to_s = lax.optimization_barrier(
+        (got_a, enc_a, enc_c, map_a, map_c, to_c, to_t, gh, base_c, to_s)
     )
     sent_c, query = messages(
         cap_e,
@@ -607,20 +599,20 @@
     qk, m, a = attend(got_a, enc_a, map_a, query, w_keyval)
     return finish(
         got_c,
+        qk,
+        m,
+        a,
         enc_c,
         map_c,
-        qk,
-        hits,
-        inv,
+        to_c,
+        to_t,
         gru_input,
         gru_bias,
         gh,
         old,
-        m,
-        a,
+        memory,
         w_keyval,
         w_out,
-        memory,
         to_s,
     )
 

time: 139 us -> 138 us (level)
  Pallas kernels: 50.5 us -> 48.6 us
  transfers between devices with their start and end apart: 2 -> 2, of which waited for: 2 -> 2; matrix products, arithmetic and copies ran while one was open for 12% -> 13% of each run, Pallas kernels for 21% -> 20%
where the time goes in v4:
time: 138 us
  Pallas kernels  48.6 us (35%)
  waiting for transfers between devices  37.6 us (27%)
  blocking collectives  21 us (15%)
  other arithmetic  13.2 us (10%)
  starting transfers between devices  11.9 us (9%)
  local copies, waits for them, and re-layouts  4.77 us (3%)
    all_to_all x2, waiting for transfers between devices, exchange(): return lax.all_to_all(x, AXES, split_axis=0, concat_axis=0, tiled=True)  37.6 us
    all_to_all x1, blocking collectives, exchange(): return lax.all_to_all(x, AXES, split_axis=0, concat_axis=0, tiled=True)  21 us
    pallas_call x1, Pallas kernels, attend(): pl.pallas_call(attend_kernel, out_shape=tuple((pltpu.VMEM(*x) for x in sh...  17 us
    pallas_call x3, Pallas kernels, pick(): pl.pallas_call(functools.partial(pick_kernel, cols, static), out_shape=pl...  14.1 us
    convert_element_type x3, other arithmetic, encode(): return jnp.cos(dt[..., None] * freq + phase).astype(BF16)  13.2 us
    all_to_all x2, starting transfers between devices, exchange(): return lax.all_to_all(x, AXES, split_axis=0, concat_axis=0, tiled=True)  11.9 us
    pallas_call x1, Pallas kernels, finish(): pl.pallas_call(finish_kernel, out_shape=(pltpu.HBM(emb_shape, BF16), pltp...  7.16 us
    pallas_call x1, Pallas kernels, messages(): pl.pallas_call(functools.partial(message_kernel, cap_e), out_shape=(pltpu...  4.46 us
  transfers between devices with their start and end apart: 2, of which 2 were waited for; matrix products, arithmetic and copies ran while one was open for 13% of the time, Pallas kernels for 20%

profile of v4, /device:TPU:1, one launch (start us, length us, event | category | flops | bytes accessed | tf_op | source)
XLA Modules:
  0.0 137.9 jit_solution(4608510653719005758)
XLA Ops:
  0.6 2.2 %shard_map.176 = (s32[128,128]{1,0:T(8,128)S(1)}, s32[128,128]{1,0:T(8,128)S(1)}, f32[128,128]{1,0:T(8,128)S(1)}) custom-call(s32[20,128]{1,0:T(8,128)} %bitcast.31, s32[20,128]{1,0:T(8,128)} %bitcast.32, s32[2,128]{1,0:T(2,128)} %bitcast.37, s32[1,128]{1,0:T(1,128)} %bitcast.38), custom_call_target="tpu_custom_call" | custom-call | tf_op jit(solution)/shard_map/pallas_call | solution.py:29
  2.8 21.0 %all_to_all.28 = s32[128,1,128]{2,1,0:T(1,128)} all-to-all(s32[128,1,128]{2,1,0:T(1,128)S(1)} %bitcast.24), channel_id=1, replica_groups=mesh['grp'=4,'dev'=32] {'grp','dev'}, dimensions={0} | all-to-all | bytes 131072 | tf_op jit(solution)/shard_map/all_to_all | solution.py:25
  23.8 7.0 %shard_map.177 = bf16[5120,512]{1,0:T(8,128)(2,1)} custom-call(s32[128,128]{1,0:T(8,128)} %bitcast.27, bf16[2048,512]{1,0:T(8,128)(2,1)} %refs_12_.1), custom_call_target="tpu_custom_call" | custom-call | tf_op jit(solution)/shard_map/pallas_call | solution.py:206
  30.8 0.0 copy-start.4
  30.8 0.0 copy-start.2
  30.8 5.8 %all-to-all-start.1 = ((bf16[128,40,512]{2,1,0:T(8,128)(2,1)}), bf16[128,40,512]{2,1,0:T(8,128)(2,1)}, u32[]{:S(2)}, u32[]{:S(2)}) async-start(bf16[128,40,512]{2,1,0:T(8,128)(2,1)} %bitcast.25), calls=%async_computation.1 | async-start | bytes 10485760 | tf_op jit(solution)/shard_map/all_to_all | solution.py:25
  36.6 0.1 concatenate.12
  36.7 0.1 mul.45
  36.8 0.1 slice_bitcast_fusion.1
  36.9 0.1 copy.23
  36.9 0.1 concatenate.13
  37.0 0.7 reshape.55.map_ref
  37.8 0.1 fusion
  37.9 0.6 copy.24
  38.5 0.7 reshape.62.refs_2_
  39.2 0.9 cosine_convert_fusion.2.refs_3_
  40.1 1.6 %cosine_convert_fusion.1.refs_4_ = bf16[512,128]{1,0:T(8,128)(2,1)} fusion(f32[128]{0:T(128)S(1)} %copy-done.2, f32[128]{0:T(128)S(1)} %copy-done.3, f32[512]{0:T(512)S(1)} %bitcast.33), kind=kLoop, calls=%fused_computation.1 | loop fusion | flops 196608 | bytes 134144 | tf_op jit(solution)/shard_map/convert_element_type | solution.py:513
  41.7 10.7 %cosine_convert_fusion.enc_ref = bf16[5120,128]{1,0:T(8,128)(2,1)} fusion(f32[128]{0:T(128)S(1)} %copy-done.2, f32[128]{0:T(128)S(1)} %copy-done.3, f32[5120]{0:T(1024)S(1)} %mul.45), kind=kLoop, calls=%fused_computation | loop fusion | flops 1966080 | bytes 1332224 | tf_op jit(solution)/shard_map/convert_element_type | solution.py:513
  52.4 0.1 slice.24
  52.5 0.7 reshape.57.refs_6_
  53.2 3.2 %shard_map.178.old_ref.refs_11_ = bf16[512,512]{1,0:T(8,128)(2,1)} custom-call(s32[128,128]{1,0:T(8,128)} %bitcast.28, bf16[2048,512]{1,0:T(8,128)(2,1)} %refs_12_.1), custom_call_target="tpu_custom_call" | custom-call | tf_op jit(solution)/shard_map/pallas_call | solution.py:206
  56.4 3.9 %shard_map.180 = bf16[1024,512]{1,0:T(8,128)(2,1)} custom-call(s32[128,128]{1,0:T(8,128)} %bitcast.29, bf16[2048,512]{1,0:T(8,128)(2,1)} %refs_12_.1), custom_call_target="tpu_custom_call" | custom-call | tf_op jit(solution)/shard_map/pallas_call | solution.py:206
  60.3 0.0 copy-start
  60.3 0.7 reshape.60.refs_15_
  61.0 0.7 reshape.58.refs_7_
  61.7 3.7 %shard_map.179.refs_10_ = bf16[512,1536]{1,0:T(8,128)(2,1)} custom-call(bf16[512,512]{1,0:T(8,128)(2,1)} %shard_map.178.old_ref.refs_11_, bf16[512,1536]{1,0:T(8,128)(2,1)} %wh_ref.1, f32[2,1536]{1,0:T(2,128)} %refs_9_.1), custom_call_target="tpu_custom_call" | custom-call | tf_op jit(solution)/shard_map/pallas_call | solution.py:307
  65.4 35.6 %all-to-all-done.1 = bf16[128,40,512]{2,1,0:T(8,128)(2,1)} async-done(((bf16[128,40,512]{2,1,0:T(8,128)(2,1)}), bf16[128,40,512]{2,1,0:T(8,128)(2,1)}, u32[]{:S(2)}, u32[]{:S(2)}) %all-to-all-start.1) | async-done | bytes 5242912 | tf_op jit(solution)/shard_map/all_to_all | solution.py:25
  100.9 4.5 %shard_map.181 = (bf16[128,8,512]{2,1,0:T(8,128)(2,1)}, bf16[128,512]{1,0:T(8,128)(2,1)}) custom-call(bf16[1152,1024]{1,0:T(8,128)(2,1)S(1)} %copy-done, bf16[128,40,512]{2,1,0:T(8,128)(2,1)} %bitcast.14.refs_1_, s32[1,1024]{1,0:T(1,128)} %reshape.62.refs_2_, bf16[128,128]{1,0:T(8,128)(2,1)} %cosine_convert_fusion.2.refs_3_, f32[1,1024]{1,0:T(1,128)} %bitcast.35, ...), custom_call_target="tpu_custom_call" | custom-call | tf_op jit(solution)/shard_map/pallas_call | solution.py:290
  105.4 6.2 %all-to-all-start.2 = ((bf16[128,8,512]{2,1,0:T(8,128)(2,1)}), bf16[128,8,512]{2,1,0:T(8,128)(2,1)S(1)}, u32[]{:S(2)}, u32[]{:S(2)}) async-start(bf16[128,8,512]{2,1,0:T(8,128)(2,1)} %get-tuple-element.25), calls=%async_computation.2 | async-start | bytes 2097152 | tf_op jit(solution)/shard_map/all_to_all | solution.py:25
  111.6 17.0 %shard_map.182 = (bf16[512,640]{1,0:T(8,128)(2,1)S(1)}, f32[512,128]{1,0:T(8,128)S(1)}, f32[512,768]{1,0:T(8,128)S(1)}) custom-call(bf16[5120,512]{1,0:T(8,128)(2,1)} %bitcast.8.rows_ref, bf16[5120,128]{1,0:T(8,128)(2,1)} %cosine_convert_fusion.enc_ref, s32[1,5120]{1,0:T(1,128)} %reshape.55.map_ref, bf16[128,512]{1,0:T(8,128)(2,1)} %get-tuple-element.28.q_ref, ...), custom_call_target="tpu_custom_call" | custom-call | tf_op jit(solution)/shard_map/pallas_call | solution.py:370
  128.6 2.0 %all-to-all-done.2.refs_0_ = bf16[128,8,512]{2,1,0:T(8,128)(2,1)S(1)} async-done(((bf16[128,8,512]{2,1,0:T(8,128)(2,1)}), bf16[128,8,512]{2,1,0:T(8,128)(2,1)S(1)}, u32[]{:S(2)}, u32[]{:S(2)}) %all-to-all-start.2) | async-done | bytes 1048608 | tf_op jit(solution)/shard_map/all_to_all | solution.py:25
  130.6 7.2 %shard_map.183 = (bf16[128,512]{1,0:T(8,128)(2,1)}, bf16[2048,512]{1,0:T(8,128)(2,1)}) custom-call(bf16[128,8,512]{2,1,0:T(8,128)(2,1)S(1)} %all-to-all-done.2.refs_0_, bf16[512,640]{1,0:T(8,128)(2,1)S(1)} %get-tuple-element.29.refs_1_, f32[512,128]{1,0:T(8,128)S(1)} %get-tuple-element.30.refs_2_, f32[512,768]{1,0:T(8,128)S(1)} %get-tuple-element.31.refs_3_, ...), custom_call_target="tpu_custom_call" | custom-call | tf_op jit(solution)/shard_map/pallas_call | solution.py:502
  (10 shorter events, 0.0 us)
Async XLA Ops:
  30.8 5.8 %copy-start.4 = (s32[128]{0:T(128)S(1)}, s32[128]{0:T(128)}, u32[]{:S(2)}) copy-start(s32[128]{0:T(128)} %param.19) | copy-start | bytes 1540
  30.8 8.4 %copy-start.2 = (f32[128]{0:T(128)S(1)}, f32[128]{0:T(128)}, u32[]{:S(2)}) copy-start(f32[128]{0:T(128)} %param.23) | copy-start | bytes 1540
  30.8 8.4 %copy-start.3 = (f32[128]{0:T(128)S(1)}, f32[128]{0:T(128)}, u32[]{:S(2)}) copy-start(f32[128]{0:T(128)} %param.22) | copy-start | bytes 1540
  30.8 70.1 %all-to-all-start.1 = ((bf16[128,40,512]{2,1,0:T(8,128)(2,1)}), bf16[128,40,512]{2,1,0:T(8,128)(2,1)}, u32[]{:S(2)}, u32[]{:S(2)}) async-start(bf16[128,40,512]{2,1,0:T(8,128)(2,1)} %bitcast.25), calls=%async_computation.1 | async-start | bytes 10485760 | tf_op jit(solution)/shard_map/all_to_all | solution.py:25
  36.6 15.8 %copy-start.1 = (s32[128,1,128]{2,1,0:T(1,128)S(1)}, s32[128,1,128]{2,1,0:T(1,128)}, u32[]{:S(2)}) copy-start(s32[128,1,128]{2,1,0:T(1,128)} %all_to_all.28) | copy-start | bytes 196612
  60.3 40.6 %copy-start = (bf16[1152,1024]{1,0:T(8,128)(2,1)S(1)}, bf16[1152,1024]{1,0:T(8,128)(2,1)}, u32[]{:S(2)}) copy-start(bf16[1152,1024]{1,0:T(8,128)(2,1)} %refs_0_.1) | copy-start | bytes 7077892
  105.4 25.2 %all-to-all-start.2 = ((bf16[128,8,512]{2,1,0:T(8,128)(2,1)}), bf16[128,8,512]{2,1,0:T(8,128)(2,1)S(1)}, u32[]{:S(2)}, u32[]{:S(2)}) async-start(bf16[128,8,512]{2,1,0:T(8,128)(2,1)} %get-tuple-element.25), calls=%async_computation.2 | async-start | bytes 2097152 | tf_op jit(solution)/shard_map/all_to_all | solution.py:25
